TPU v7x, 32 devices: a whole 2x2x4 slice. The times are simulated.
32 devices in a mesh: liq: 4 (over y, x), ill: 2 (over core), dur: 4 (over z).
Axes of the slice: x: 2, y: 2, z: 4, core: 2. Of those that a mesh axis runs over, the one named last changes fastest.
Arguments:
- marginal_value: float32 [32, 8, 4, 512], P(None, 'dur', 'ill', 'liq'), may hold values from 0.5 to 2
- transition: float32 [32, 32], replicated, may hold values from 0 to 1, as said below
- discount_shock: float32 [32], replicated, may hold values from 0.5 to 2
- illiquid_drift: float32 [4], P('ill'), may hold values from 0.2 to 0.8
- durable_keep: float32 [8], P('dur'), may hold values from 0.3 to 0.9
- bracket_index: int32 [32, 8, 4, 512], P(None, 'dur', 'ill', 'liq'), may hold values from 0 to 510
- bracket_weight: float32 [32, 8, 4, 512], P(None, 'dur', 'ill', 'liq'), may hold values from 0 to 1
- steady_consumption: float32 [32, 8, 4, 512], P(None, 'dur', 'ill', 'liq'), may hold values from 0.8 to 1.6
- lottery_weight: float32 [32, 8, 4, 512], P(None, 'dur', 'ill', 'liq'), may hold values from 0 to 1
- liquid_target: int32 [32, 8, 4, 512], P(None, 'dur', 'ill', 'liq'), may hold values from 0 to 510
- illiquid_target: int32 [32, 8, 4], P(None, 'dur', 'ill'), may hold values from 0 to 3
- population: float32 [32, 8, 4, 512], P(None, 'dur', 'ill', 'liq'), may hold values from 0.5 to 2
Outputs:
- consumption: float32 [32, 8, 4, 512], P(None, 'dur', 'ill', 'liq')
- population_next: float32 [32, 8, 4, 512], P(None, 'dur', 'ill', 'liq')
Inputs may be any that keep to these rules, and one draw needn't show every extreme that they name: `bracket_index`: global liquid index; the upper bracket point is index + 1. `liquid_target`: global liquid index; the upper target is index + 1. `illiquid_target`: global illiquid index. `transition`: entries positive, every row sums to one.
All inputs are finite; a program needn't handle non-finite values.
Results may differ from a plain program's by a relative error of at most 0.000065.
Values sent between devices are 32-bit elements; how exact they have to be, the bound alone decides.
A program may use at most 64 MiB of HBM per device.

v0:
```python
import functools

import jax
import jax.numpy as jnp
from jax import lax
from jax.experimental import pallas as pl
from jax.experimental.pallas import tpu as pltpu
from jax.sharding import PartitionSpec as P

DISCOUNT = 0.96
GROSS_RATE = 1.01
SLOPE_GAIN = 0.5
HIGHEST_PREC = lax.Precision.HIGHEST
MESH_ID = pl.DeviceIdType.MESH
NT = (((1,), (1,)), ((), ()))
TILE = 8


def split_by(x, n):
    if n & (n - 1) == 0:
        return x >> (n.bit_length() - 1), x & (n - 1)
    return lax.div(x, jnp.int32(n)), lax.rem(x, jnp.int32(n))


def dot(a, b):
    return jnp.dot(a, b, precision=HIGHEST_PREC, preferred_element_type=jnp.float32)


def iota(shape, axis):
    return lax.broadcasted_iota(jnp.int32, shape, axis)


def as_float(flag):
    return jnp.where(flag, jnp.float32(1.0), jnp.float32(0.0))


def peer_of(me, step, n):
    if n & (n - 1):
        return lax.rem(me + step, n)
    out = me
    for bit in range(n.bit_length() - 1):
        if step >> bit & 1:
            out = out + (1 - 2 * lax.rem(lax.div(me, jnp.int32(1 << bit)), jnp.int32(2))) * (1 << bit)
    return out


def kernel(
    dims,
    value_hbm, transition_hbm, shock_hbm, drift_hbm, keep_hbm, index_hbm, weight_hbm,
    steady_hbm, lottery_hbm, target_hbm, ill_target_hbm, population_hbm,
    consumption_ref, next_ref,
    value_ref, transition_ref, shock_ref, index_ref, weight_ref, steady_ref, lottery_ref, target_ref,
    population_ref, drift_ref, keep_ref, ill_target_ref, load_sem,
    first_mat, first_up, second_mat, second_up, next_mat, next_in,
    near_value, value_two, pencil, mass_low, mass_high, target_hi, target_lo,
    placed_rows, terms, terms_in, owner_sum, owner_in, settled, depart, depart_in,
    value_send, value_recv, pencil_send, pencil_recv, terms_send, terms_recv,
    owner_send, owner_recv, depart_send, depart_recv,
):
    incomes, durables, ill_rows, liq_rows, liq_n, ill_n, dur_n = dims
    group = durables * ill_rows
    rows = incomes * group
    half_rows = rows // 2
    plane_rows = incomes * ill_rows
    liq_me, ill_me, dur_me = (lax.axis_index(name) for name in ("liq", "ill", "dur"))
    far_first = range(liq_n - 1, 0, -1)

    barrier = pltpu.get_barrier_semaphore()
    for step in far_first:
        pl.semaphore_signal(barrier, inc=1, device_id={"liq": peer_of(liq_me, step, liq_n)}, device_id_type=MESH_ID)
    for step in range(1, ill_n):
        pl.semaphore_signal(barrier, inc=1, device_id={"ill": peer_of(ill_me, step, ill_n)}, device_id_type=MESH_ID)

    @pl.when(dur_me > 0)
    def _():
        pl.semaphore_signal(barrier, inc=1, device_id={"dur": dur_me - 1}, device_id_type=MESH_ID)

    @pl.when(dur_me < dur_n - 1)
    def _():
        pl.semaphore_signal(barrier, inc=1, device_id={"dur": dur_me + 1}, device_id_type=MESH_ID)

    loads = [
        pltpu.make_async_copy(source, held, load_sem.at[slot])
        for slot, (source, held) in enumerate((
            (transition_hbm, transition_ref), (shock_hbm, shock_ref), (drift_hbm, drift_ref), (value_hbm, value_ref),
            (keep_hbm, keep_ref), (ill_target_hbm, ill_target_ref),
            (index_hbm, index_ref), (weight_hbm, weight_ref), (target_hbm, target_ref),
            (lottery_hbm, lottery_ref), (steady_hbm, steady_ref), (population_hbm, population_ref),
        ))
    ]
    for load in loads:
        load.start()
    for load in loads[:3]:
        load.wait()

    transition = transition_ref[...]
    row_z, row_rest = split_by(iota((rows, rows), 0), group)
    col_z, col_rest = split_by(iota((rows, rows), 1), group)
    row_d, row_a = split_by(row_rest, ill_rows)
    col_d, col_a = split_by(col_rest, ill_rows)
    spread = as_float(split_by(iota((rows, incomes), 0), group)[0] == iota((rows, incomes), 1))
    spread_t = as_float(iota((incomes, rows), 0) == split_by(iota((incomes, rows), 1), group)[0])
    drift = jnp.zeros((rows, rows), jnp.float32)
    for a in range(ill_rows):
        drift = jnp.where(row_a == a, drift_ref[a], drift)
    is_last = as_float(ill_me == ill_n - 1)
    same_d = row_d == col_d
    top_row = row_a == ill_rows - 1
    local = jnp.where(col_a == row_a, drift, 0.0)
    local = local + jnp.where(col_a == row_a + 1, 1.0 - drift, 0.0)
    local = local + jnp.where(top_row & (col_a == ill_rows - 1), is_last * (1.0 - drift), 0.0)
    local = jnp.where(same_d, local, 0.0)
    upper = jnp.where(same_d & top_row & (col_a == 0), (1.0 - is_last) * (1.0 - drift), 0.0)
    constant = jnp.float32(DISCOUNT * GROSS_RATE)
    eye = iota((incomes, incomes), 0) == iota((incomes, incomes), 1)
    scaled = dot(jnp.where(eye, constant * shock_ref[...], 0.0), transition)
    wide = dot(dot(spread, scaled), spread_t)
    first_mat[...] = wide * local
    first_up[...] = wide * upper

    dur_peers = jnp.minimum(dur_me, 1) + jnp.minimum(dur_n - 1 - dur_me, 1)
    pl.semaphore_wait(barrier, liq_n - 1 + ill_n - 1 + dur_peers)

    ill_below = lax.rem(ill_me + ill_n - 1, ill_n)

    def value_copy(k, source):
        return pltpu.make_async_remote_copy(
            src_ref=source, dst_ref=near_value.at[k], send_sem=value_send.at[k],
            recv_sem=value_recv.at[k], device_id={"ill": ill_below}, device_id_type=MESH_ID,
        )

    def pencil_copy(k, half, step):
        slot = (k * 2 + half) * liq_n + step
        part = pencil.at[k * liq_n + liq_me, pl.ds(half * half_rows, half_rows)]
        return pltpu.make_async_remote_copy(
            src_ref=part, dst_ref=part, send_sem=pencil_send.at[slot], recv_sem=pencil_recv.at[slot],
            device_id={"liq": peer_of(liq_me, step, liq_n)}, device_id_type=MESH_ID,
        )

    def pencil_relay(half):
        near, far = (1, 2) if half == 0 else (2, 1)
        slot = (2 + half) * liq_n
        part = pencil.at[liq_n + peer_of(liq_me, near, liq_n), pl.ds(half * half_rows, half_rows)]
        return pltpu.make_async_remote_copy(
            src_ref=part, dst_ref=part, send_sem=pencil_send.at[slot], recv_sem=pencil_recv.at[slot],
            device_id={"liq": peer_of(liq_me, far, liq_n)}, device_id_type=MESH_ID,
        )

    relayed = liq_n == 4
    if relayed:
        early, late = [(0, 1), (1, 2)], [(1, 1), (0, 2)]
    else:
        early, late = [(0, step) for step in far_first], [(1, step) for step in far_first]

    def terms_copy(d, step):
        peer = peer_of(ill_me, step, ill_n)
        slot = d * (ill_n - 1) + step - 1
        return pltpu.make_async_remote_copy(
            src_ref=terms.at[pl.ds((d * ill_n + peer) * (liq_n * plane_rows), liq_n * plane_rows)],
            dst_ref=terms_in.at[slot], send_sem=terms_send.at[slot], recv_sem=terms_recv.at[slot],
            device_id={"ill": peer}, device_id_type=MESH_ID,
        )

    def owner_copy(d, step):
        peer = peer_of(liq_me, step, liq_n)
        slot = d * (liq_n - 1) + step - 1
        return pltpu.make_async_remote_copy(
            src_ref=owner_sum.at[d * liq_n + peer], dst_ref=owner_in.at[slot],
            send_sem=owner_send.at[slot], recv_sem=owner_recv.at[slot],
            device_id={"liq": peer}, device_id_type=MESH_ID,
        )

    loads[3].wait()
    value_copy(0, value_ref).start()
    drifted = dot(first_mat[...], value_ref[...])
    value_copy(0, value_ref).wait_recv()
    drifted = drifted + dot(first_up[...], near_value[0])
    pencil[liq_me] = lax.rsqrt(drifted)
    for half in range(2):
        for step in far_first:
            pencil_copy(0, half, step).start()

    wide = constant * dot(dot(spread, transition), spread_t)
    second_mat[...] = wide * local
    second_up[...] = wide * upper

    for load in loads[4:]:
        load.wait()

    first_d = as_float(dur_me == 0)
    stay = [keep_ref[d] for d in range(durables)]
    stay[0] = first_d + (1.0 - first_d) * stay[0]
    back_d, back_rest = split_by(iota((rows, rows), 1), plane_rows)
    back_a = split_by(back_rest, ill_rows)[1]
    stays = jnp.zeros((rows, rows), jnp.float32)
    for d in range(durables):
        stays = jnp.where(back_d == d, stay[d], stays)
    mix = jnp.where(back_d == row_d, stays, 0.0) + jnp.where(back_d == row_d + 1, 1.0 - stays, 0.0)
    mix = jnp.where(back_a == row_a, mix, 0.0)
    back_z = split_by(split_by(iota((incomes, rows), 1), plane_rows)[1], ill_rows)[0]
    turned = lax.dot_general(spread, transition, NT, precision=HIGHEST_PREC, preferred_element_type=jnp.float32)
    wide = dot(turned, as_float(iota((incomes, rows), 0) == back_z))
    next_mat[...] = wide * mix
    in_z, in_a = split_by(iota((incomes, plane_rows), 1), ill_rows)
    wide = dot(turned, as_float(iota((incomes, plane_rows), 0) == in_z))
    in_row = split_by(iota((rows, plane_rows), 0), group)[1]
    in_row_d, in_row_a = split_by(in_row, ill_rows)
    in_col_a = split_by(iota((rows, plane_rows), 1), ill_rows)[1]
    next_in[...] = jnp.where((in_row_d == durables - 1) & (in_row_a == in_col_a), wide, 0.0)

    def block_of(position):
        block = jnp.zeros(position.shape, jnp.int32)
        for h in range(1, liq_n):
            block = block + jnp.where(position >= h * liq_rows, 1, 0)
        return block, position - block * liq_rows

    target_hi[...], lo = block_of(target_ref[...])
    target_lo[...] = lo.astype(jnp.float32)

    def interpolate(k, tile):
        span = pl.ds(tile * TILE, TILE)
        index = index_ref[span, :]
        low_block, low_lane = block_of(index)
        high_block, high_lane = block_of(index + 1)
        low = high = None
        for h in range(liq_n):
            block = pencil[k * liq_n + h, span, :]
            low_h = jnp.take_along_axis(block, low_lane, axis=1, mode="promise_in_bounds")
            high_h = jnp.take_along_axis(block, high_lane, axis=1, mode="promise_in_bounds")
            low = low_h if h == 0 else jnp.where(low_block == h, low_h, low)
            high = high_h if h == 0 else jnp.where(high_block == h, high_h, high)
        weight = weight_ref[span, :]
        return weight * low + (1.0 - weight) * high

    tiles = rows // TILE
    halves = (range(tiles // 2), range(tiles // 2, tiles))

    def first_policy(half):
        for step in far_first:
            pencil_copy(0, half, step).wait_recv()
        for tile in halves[half]:
            span = pl.ds(tile * TILE, TILE)
            chosen = interpolate(0, tile)
            value_two[span, :] = GROSS_RATE / (chosen * chosen)
            share = jnp.clip(lottery_ref[span, :] + SLOPE_GAIN * (chosen - steady_ref[span, :]), 0.0, 1.0)
            mass = population_ref[span, :]
            mass_low[span, :] = mass * share
            mass_high[span, :] = mass * (1.0 - share)

    lanes = 2 * liq_n
    sub = iota((lanes, liq_rows), 0)
    lane_at = iota((TILE, liq_rows), 1)
    sub_block = jnp.where(sub < liq_n, sub, sub - liq_n)
    lane_row = iota((liq_rows, liq_rows), 0).astype(jnp.float32).astype(jnp.bfloat16)
    one = jnp.ones((liq_rows, liq_rows), jnp.bfloat16)
    nil = jnp.zeros((liq_rows, liq_rows), jnp.bfloat16)
    per_tile = TILE // group

    def scatter_tile(d, tile):
        span = pl.ds(pl.multiple_of(tile * TILE, TILE), TILE)
        low_t, high_t, hi_t, lo_t = mass_low[span, :], mass_high[span, :], target_hi[span, :], target_lo[span, :]
        for zz in range(per_tile):
            z = tile * per_tile + zz
            totals = []
            for a in range(ill_rows):
                k = zz * group + d * ill_rows + a
                both = jnp.where(sub < liq_n, low_t[k : k + 1, :], high_t[k : k + 1, :])
                both = jnp.where(hi_t[k : k + 1, :] == sub_block, both, 0.0)
                rounded = both.astype(jnp.bfloat16).astype(jnp.float32)
                parts = jnp.concatenate([both, both - rounded], axis=0).astype(jnp.bfloat16)
                place = jnp.broadcast_to(lo_t[k : k + 1, :], (2 * TILE, liq_rows)).astype(jnp.bfloat16)
                place = jnp.concatenate([place] * (liq_rows // (2 * TILE)), axis=0)
                hot = jnp.where(lane_row == place, one, nil)
                placed = lax.dot_general(parts, hot, NT, preferred_element_type=jnp.float32)
                placed = placed[:lanes] + placed[lanes:]
                totals.append(placed)
            for dest in range(ill_n * ill_rows):
                out = None
                for a in range(ill_rows):
                    here = as_float(ill_target_ref[d * ill_rows + a, z] == dest) * totals[a]
                    out = here if out is None else out + here
                base = dest // ill_rows * lanes * plane_rows + z * ill_rows + dest % ill_rows
                placed_rows[pl.ds(base, lanes, stride=plane_rows), :] = out

    unroll = tiles // 2

    def scatter(d, half):
        def step(pair, carry):
            for turn in range(unroll):
                scatter_tile(d, halves[half].start + unroll * pair + turn)
            return carry

        lax.fori_loop(0, tiles // 2 // unroll, step, 0)

    def send_terms(d):
        for owner in range(ill_n):
            for piece in range(plane_rows // TILE):
                carried = None
                for h in range(liq_n):
                    low_at = (owner * lanes + h) * plane_rows + piece * TILE
                    low = placed_rows[pl.ds(low_at, TILE), :]
                    moved = pltpu.roll(placed_rows[pl.ds(low_at + liq_n * plane_rows, TILE), :], 1, 1)
                    edge = jnp.where(lane_at > 0, moved, 0.0 if carried is None else carried)
                    carried = moved
                    out_at = ((d * ill_n + owner) * liq_n + h) * plane_rows + piece * TILE
                    terms[pl.ds(out_at, TILE), :] = low + edge
        for step in range(1, ill_n):
            terms_copy(d, step).start()

    def send_owners(d):
        for step in range(1, ill_n):
            terms_copy(d, step).wait_recv()
        for h in range(liq_n):
            start = pl.multiple_of(((d * ill_n + ill_me) * liq_n + h) * plane_rows, TILE)
            total = terms[pl.ds(start, plane_rows), :]
            for step in range(1, ill_n):
                total = total + terms_in[d * (ill_n - 1) + step - 1, pl.ds(h * plane_rows, plane_rows), :]
            owner_sum[d * liq_n + h] = total
        for step in far_first:
            owner_copy(d, step).start()

    def collect(d):
        for step in far_first:
            owner_copy(d, step).wait_recv()
        total = owner_sum[d * liq_n + liq_me]
        for step in range(1, liq_n):
            total = total + owner_in[d * (liq_n - 1) + step - 1]
        settled[pl.ds(d * plane_rows, plane_rows), :] = total
        return total

    def second_policy():
        if relayed:
            for half in range(2):
                pencil_relay(half).wait_recv()
        else:
            for half, step in early:
                pencil_copy(1, half, step).wait_recv()
        for half, step in late:
            pencil_copy(1, half, step).wait_recv()
        for tile in range(tiles):
            consumption_ref[pl.ds(tile * TILE, TILE), :] = interpolate(1, tile)

    first_policy(0)
    scatter(0, 0)
    first_policy(1)
    value_copy(1, value_two).start()
    scatter(0, 1)
    send_terms(0)
    value_copy(1, value_two).wait_recv()
    drifted = dot(second_mat[...], value_two[...]) + dot(second_up[...], near_value[1])
    pencil[liq_n + liq_me] = lax.rsqrt(drifted)
    for half, step in early:
        pencil_copy(1, half, step).start()
    for d in range(1, durables):
        scatter(d, 0)
        if d == 1:
            send_owners(0)
            for half, step in late:
                pencil_copy(1, half, step).start()
        scatter(d, 1)
        send_terms(d)
    for d in range(1, durables):
        send_owners(d)
    if relayed:
        for half, step in early:
            pencil_copy(1, half, step).wait_recv()
        for half in range(2):
            pencil_relay(half).start()

    depart_copy = pltpu.make_async_remote_copy(
        src_ref=depart, dst_ref=depart_in, send_sem=depart_send.at[0], recv_sem=depart_recv.at[0],
        device_id={"dur": jnp.maximum(dur_me - 1, 0)}, device_id_type=MESH_ID,
    )

    depart[...] = (1.0 - stay[0]) * collect(0)

    @pl.when(dur_me > 0)
    def _():
        depart_copy.start()

    for d in range(1, durables):
        collect(d)
    next_ref[...] = dot(next_mat[...], settled[...])
    second_policy()

    @pl.when(dur_me < dur_n - 1)
    def _():
        depart_copy.wait_recv()
        next_ref[...] += dot(next_in[...], depart_in[...])

    value_copy(0, value_ref).wait_send()
    value_copy(1, value_two).wait_send()
    for step in range(1, liq_n):
        for half in range(2):
            pencil_copy(0, half, step).wait_send()
        for d in range(durables):
            owner_copy(d, step).wait_send()
    for half, step in early + late:
        pencil_copy(1, half, step).wait_send()
    if relayed:
        for half in range(2):
            pencil_relay(half).wait_send()
    for step in range(1, ill_n):
        for d in range(durables):
            terms_copy(d, step).wait_send()

    @pl.when(dur_me > 0)
    def _():
        depart_copy.wait_send()


def store(consumption_ref, next_ref, consumption_hbm, next_hbm, sem):
    copies = [
        pltpu.make_async_copy(consumption_ref, consumption_hbm, sem.at[0]),
        pltpu.make_async_copy(next_ref, next_hbm, sem.at[1]),
    ]
    for copy in copies:
        copy.start()
    for copy in copies:
        copy.wait()


def body(
    marginal_value,
    transition,
    discount_shock,
    illiquid_drift,
    durable_keep,
    bracket_index,
    bracket_weight,
    steady_consumption,
    lottery_weight,
    liquid_target,
    illiquid_target,
    population,
):
    shape = marginal_value.shape
    incomes, durables, ill_rows, liq_rows = shape
    liq_n, ill_n, dur_n = (lax.axis_size(name) for name in ("liq", "ill", "dur"))
    rows = incomes * durables * ill_rows
    plane_rows = incomes * ill_rows
    flat = lambda x: x.reshape(rows, liq_rows)
    anywhere = pl.BlockSpec(memory_space=pl.ANY)
    f32 = jnp.float32
    block = (rows, liq_rows)
    dma = pltpu.SemaphoreType.DMA
    vmem = pl.BlockSpec(memory_space=pltpu.VMEM)
    held = pltpu.VMEM(block, f32)
    result = jax.ShapeDtypeStruct(block, f32)
    dims = (incomes, durables, ill_rows, liq_rows, liq_n, ill_n, dur_n)
    outs = pl.pallas_call(
        functools.partial(kernel, dims),
        out_shape=(held, held),
        in_specs=[anywhere] * 12,
        out_specs=(vmem, vmem),
        scratch_shapes=[
            pltpu.VMEM(block, f32),
            pltpu.VMEM((incomes, incomes), f32),
            pltpu.VMEM((1, incomes), f32),
            pltpu.VMEM(block, jnp.int32),
            pltpu.VMEM(block, f32),
            pltpu.VMEM(block, f32),
            pltpu.VMEM(block, f32),
            pltpu.VMEM(block, jnp.int32),
            pltpu.VMEM(block, f32),
            pltpu.SMEM((ill_rows,), f32),
            pltpu.SMEM((durables,), f32),
            pltpu.SMEM((durables * ill_rows, incomes), jnp.int32),
            dma((12,)),
            pltpu.VMEM((rows, rows), f32),
            pltpu.VMEM((rows, rows), f32),
            pltpu.VMEM((rows, rows), f32),
            pltpu.VMEM((rows, rows), f32),
            pltpu.VMEM((rows, rows), f32),
            pltpu.VMEM((rows, plane_rows), f32),
            pltpu.VMEM((2,) + block, f32),
            pltpu.VMEM(block, f32),
            pltpu.VMEM((2 * liq_n,) + block, f32),
            pltpu.VMEM(block, f32),
            pltpu.VMEM(block, f32),
            pltpu.VMEM(block, jnp.int32),
            pltpu.VMEM(block, f32),
            pltpu.VMEM((2 * ill_n * liq_n * plane_rows, liq_rows), f32),
            pltpu.VMEM((ill_n * liq_n * rows, liq_rows), f32),
            pltpu.VMEM((durables * (ill_n - 1), liq_n * plane_rows, liq_rows), f32),
            pltpu.VMEM((durables * liq_n, plane_rows, liq_rows), f32),
            pltpu.VMEM((durables * (liq_n - 1), plane_rows, liq_rows), f32),
            pltpu.VMEM(block, f32),
            pltpu.VMEM((plane_rows, liq_rows), f32),
            pltpu.VMEM((plane_rows, liq_rows), f32),
            dma((2,)),
            dma((2,)),
            dma((4 * liq_n,)),
            dma((4 * liq_n,)),
            dma((durables * (ill_n - 1),)),
            dma((durables * (ill_n - 1),)),
            dma((durables * (liq_n - 1),)),
            dma((durables * (liq_n - 1),)),
            dma((1,)),
            dma((1,)),
        ],
        compiler_params=pltpu.CompilerParams(collective_id=0, has_side_effects=True),
        name="window",
    )(
        flat(marginal_value),
        transition,
        discount_shock.reshape(1, incomes),
        illiquid_drift,
        durable_keep,
        flat(bracket_index),
        flat(bracket_weight),
        flat(steady_consumption),
        flat(lottery_weight),
        flat(liquid_target),
        jnp.transpose(illiquid_target, (1, 2, 0)).reshape(durables * ill_rows, incomes),
        flat(population),
    )
    outs = pl.pallas_call(
        store,
        out_shape=(result, result),
        in_specs=[vmem, vmem],
        out_specs=(anywhere, anywhere),
        scratch_shapes=[dma((2,))],
        name="store",
    )(*(pltpu.with_memory_space_constraint(out, pltpu.VMEM) for out in outs))
    return tuple(out.reshape(shape) for out in outs)


def solution(mesh):
    in_specs = (
        P(None, "dur", "ill", "liq"),
        P(),
        P(),
        P("ill"),
        P("dur"),
        P(None, "dur", "ill", "liq"),
        P(None, "dur", "ill", "liq"),
        P(None, "dur", "ill", "liq"),
        P(None, "dur", "ill", "liq"),
        P(None, "dur", "ill", "liq"),
        P(None, "dur", "ill"),
        P(None, "dur", "ill", "liq"),
    )
    out_specs = (P(None, "dur", "ill", "liq"), P(None, "dur", "ill", "liq"))
    return jax.shard_map(body, mesh=mesh, in_specs=in_specs, out_specs=out_specs, check_vma=False)
```

profile of v0, /device:TPU:0, one launch (start us, length us, event | category | flops | bytes accessed | tf_op | source)
XLA Modules:
  0.0 21.8 jit_solution(6120246534239686594)
XLA Ops:
  0.6 20.5 %window.1 = (f32[128,128]{1,0:T(8,128)S(1)}, f32[128,128]{1,0:T(8,128)S(1)}) custom-call(f32[128,128]{1,0:T(8,128)} %bitcast.13, f32[32,32]{1,0:T(8,128)} %transition_hbm.1, f32[1,32]{1,0:T(1,128)} %bitcast.21, f32[2]{0:T(128)} %drift_hbm.1, f32[2]{0:T(128)} %keep_hbm.1, s32[128,128]{1,0:T(8,128)} %bitcast.14, f32[128,128]{1,0:T(8,128)} %bitcast.15, ...), custom_call_target="tpu_custom_call" | custom-call | tf_op jit(solution)/shard_map/window/pallas_call | solution.py:451
  21.2 0.7 %store.1 = (f32[128,128]{1,0:T(8,128)}, f32[128,128]{1,0:T(8,128)}) custom-call(f32[128,128]{1,0:T(8,128)S(1)} %get-tuple-element.6.consumption_ref, f32[128,128]{1,0:T(8,128)S(1)} %get-tuple-element.7.next_ref), custom_call_target="tpu_custom_call" | custom-call | tf_op jit(solution)/shard_map/store/pallas_call | solution.py:518
where the time goes:
time: 22.1 us; the launch traced here: 21.8 us
  Pallas kernels  21.2 us (96%)
  between operations  0.64 us (3%)
    pallas_call x1, Pallas kernels, body(): pl.pallas_call(functools.partial(kernel, dims), out_shape=(held, held), i...  20.5 us
    pallas_call x1, Pallas kernels, body(): pl.pallas_call(store, out_shape=(result, result), in_specs=[vmem, vmem],...  0.67 us

commit v1 on v0

--- a/solution.py
+++ b/solution.py
@@ -1,3 +1,4 @@
+import contextlib
 import functools
 
 import jax
@@ -14,6 +15,10 @@
 MESH_ID = pl.DeviceIdType.MESH
 NT = (((1,), (1,)), ((), ()))
 TILE = 8
+
+
+def scope(name):
+    return contextlib.nullcontext()
 
 
 def split_by(x, n):
@@ -409,6 +414,470 @@
         depart_copy.wait_send()
 
 
+def halves_of(x):
+    high = x.astype(jnp.bfloat16)
+    return high, (x - high.astype(jnp.float32)).astype(jnp.bfloat16)
+
+
+def stack_data(x):
+    high, low = halves_of(x)
+    return jnp.concatenate([high, low, high], axis=0)
+
+
+def transposed_kernel(
+    dims,
+    value_hbm, transition_hbm, shock_hbm, drift_hbm, keep_hbm, index_hbm, weight_hbm,
+    steady_hbm, lottery_hbm, target_hbm, ill_target_hbm, population_hbm,
+    consumption_ref, next_ref,
+    value_ref, transition_ref, shock_ref, index_ref, weight_ref, steady_ref, lottery_ref, target_ref,
+    population_ref, ill_target_ref, drift_ref, keep_ref, load_sem,
+    near_out, near_in, late_out, late_in, side_out, side_in,
+    pencil_one, value_two, values_in, pencil_two, placed, mass_out, depart_out, mass_in,
+    near_send, near_recv, late_send, late_recv, side_send, side_recv,
+    value_send, value_recv, plane_send, plane_recv, mass_send, mass_recv, depart_send, depart_recv, ready_sem,
+):
+    incomes, durables, ill_rows, liq_rows, liq_n, ill_n, dur_n = dims
+    group = durables * ill_rows
+    ill_all = ill_n * ill_rows
+    part = incomes // liq_n
+    per_dest = 3 * ill_rows
+    grid_tiles = ill_rows * liq_n
+    planes = (ill_rows + 1) * liq_n
+    constant = jnp.float32(DISCOUNT * GROSS_RATE)
+    f32 = jnp.float32
+    liq_me, ill_me, dur_me = (lax.axis_index(name) for name in ("liq", "ill", "dur"))
+    peers = [(step, flip) for step in range(liq_n - 1, -1, -1) for flip in range(ill_n) if step or flip]
+
+    def at(step, flip):
+        return {"liq": peer_of(liq_me, step, liq_n), "ill": peer_of(ill_me, flip, ill_n)}
+
+    def slot_of(step, flip):
+        return flip * liq_n + step
+
+    barrier = pltpu.get_barrier_semaphore()
+    for step, flip in peers:
+        pl.semaphore_signal(barrier, inc=1, device_id=at(step, flip), device_id_type=MESH_ID)
+
+    @pl.when(dur_me > 0)
+    def _():
+        pl.semaphore_signal(barrier, inc=1, device_id={"dur": dur_me - 1}, device_id_type=MESH_ID)
+
+    @pl.when(dur_me < dur_n - 1)
+    def _():
+        pl.semaphore_signal(barrier, inc=1, device_id={"dur": dur_me + 1}, device_id_type=MESH_ID)
+
+    loads = [
+        pltpu.make_async_copy(source, held, load_sem.at[slot])
+        for slot, (source, held) in enumerate((
+            (transition_hbm, transition_ref), (shock_hbm, shock_ref), (value_hbm, value_ref),
+            (index_hbm, index_ref), (weight_hbm, weight_ref), (drift_hbm, drift_ref), (ill_target_hbm, ill_target_ref),
+            (target_hbm, target_ref), (lottery_hbm, lottery_ref), (steady_hbm, steady_ref),
+            (population_hbm, population_ref), (keep_hbm, keep_ref),
+        ))
+    ]
+    for load in loads:
+        load.start()
+
+    def rows_at(d, a, z_part):
+        return pl.ds(z_part * part * group + d * ill_rows + a, part, stride=group)
+
+    def whole_rows(d, a):
+        return pl.ds(d * ill_rows + a, incomes, stride=group)
+
+    kinds = [(d, a) for d in range(durables) for a in range(ill_rows)]
+    for load in loads[:2]:
+        load.wait()
+    transition = transition_ref[...]
+    eye = iota((incomes, incomes), 0) == iota((incomes, incomes), 1)
+    scaled = dot(jnp.where(eye, constant * shock_ref[...], 0.0), transition)
+
+    def stack_left(x):
+        high, low = halves_of(x)
+        return jnp.concatenate([high, high, low], axis=1)
+
+    def times(left, x):
+        return jnp.dot(left, stack_data(x), preferred_element_type=f32)
+
+    left_one = stack_left(scaled)
+    left_two = stack_left(constant * transition)
+    loads[2].wait()
+    wide = jnp.concatenate([value_ref[whole_rows(d, a), :] for d, a in kinds], axis=1)
+    wide = times(left_one, wide)
+    for load in loads[3:5]:
+        load.wait()
+    for k, (d, a) in enumerate(kinds):
+        for q in range(liq_n):
+            base = (d * liq_n + q) * per_dest
+            near_out[base + a] = wide[q * part : (q + 1) * part, k * liq_rows : (k + 1) * liq_rows]
+            near_out[base + ill_rows + a] = index_ref[rows_at(d, a, q), :].astype(f32)
+            near_out[base + 2 * ill_rows + a] = weight_ref[rows_at(d, a, q), :]
+
+    for load in loads[5:7]:
+        load.wait()
+    column = iota((part, incomes), 1)
+    wanted = column == liq_me * part + iota((part, incomes), 0)
+    picked = jnp.concatenate(
+        [
+            jnp.where(wanted, jnp.broadcast_to(ill_target_ref[k : k + 1, :], (part, incomes)), 0)
+            for k in range(group)
+        ],
+        axis=0,
+    )
+    spread = jnp.dot(
+        picked.astype(f32).astype(jnp.bfloat16), jnp.ones((incomes, liq_rows), jnp.bfloat16), preferred_element_type=f32
+    )
+    row = iota((TILE, liq_rows), 0)
+    drifts = jnp.zeros((TILE, liq_rows), f32)
+    for a in range(ill_rows):
+        drifts = jnp.where(row == a, drift_ref[a], drifts)
+    for k, (d, a) in enumerate(kinds):
+        side_out[d, a] = spread[k * part : (k + 1) * part]
+    for d in range(durables):
+        side_out[d, ill_rows] = drifts
+
+    with scope("bar"):
+        dur_peers = jnp.minimum(dur_me, 1) + jnp.minimum(dur_n - 1 - dur_me, 1)
+        pl.semaphore_wait(barrier, len(peers) + dur_peers)
+
+    @pl.when((dur_me < dur_n - 1) & (ill_me == 0))
+    def _():
+        pl.semaphore_signal(ready_sem, inc=1, device_id={"dur": dur_me + 1}, device_id_type=MESH_ID)
+
+    def bundle_copy(out_ref, in_ref, send, recv, step, flip):
+        there = at(step, flip)
+        return pltpu.make_async_remote_copy(
+            src_ref=out_ref.at[pl.ds((there["ill"] * liq_n + there["liq"]) * per_dest, per_dest)],
+            dst_ref=in_ref.at[pl.ds((liq_me * ill_n + ill_me) * per_dest, per_dest)],
+            send_sem=send.at[slot_of(step, flip)], recv_sem=recv.at[slot_of(step, flip)],
+            device_id=there, device_id_type=MESH_ID,
+        )
+
+    def near_copy(step, flip):
+        return bundle_copy(near_out, near_in, near_send, near_recv, step, flip)
+
+    def late_copy(step, flip):
+        return bundle_copy(late_out, late_in, late_send, late_recv, step, flip)
+
+    def side_copy(flip):
+        there = at(0, flip)
+        return pltpu.make_async_remote_copy(
+            src_ref=side_out.at[there["ill"]], dst_ref=side_in.at[ill_me],
+            send_sem=side_send.at[flip], recv_sem=side_recv.at[flip], device_id=there, device_id_type=MESH_ID,
+        )
+
+    for step, flip in peers:
+        near_copy(step, flip).start()
+    for flip in range(1, ill_n):
+        side_copy(flip).start()
+
+    for load in loads[7:]:
+        load.wait()
+    for d, a in kinds:
+        for q in range(liq_n):
+            base = (d * liq_n + q) * per_dest
+            span = rows_at(d, a, q)
+            late_out[base + a] = lottery_ref[span, :] - SLOPE_GAIN * steady_ref[span, :]
+            late_out[base + ill_rows + a] = population_ref[span, :]
+            late_out[base + 2 * ill_rows + a] = target_ref[span, :].astype(f32)
+    for step, flip in peers:
+        late_copy(step, flip).start()
+
+    own_out = (ill_me * liq_n + liq_me) * per_dest
+    own_in = (liq_me * ill_n + ill_me) * per_dest
+    for k in range(per_dest):
+        near_in[own_in + k] = near_out[own_out + k]
+        late_in[own_in + k] = late_out[own_out + k]
+    for k in range(ill_rows + 1):
+        side_in[ill_me, k] = side_out[ill_me, k]
+
+    @pl.when(ill_me == ill_n - 1)
+    def _():
+        for d in range(durables):
+            for h in range(liq_n):
+                values_in[d * planes + grid_tiles + h] = jnp.zeros((incomes, liq_rows), f32)
+
+    @pl.when(dur_me == dur_n - 1)
+    def _():
+        for a in range(ill_rows):
+            mass_in[group + a] = jnp.zeros((incomes, liq_rows), f32)
+
+    stay = [keep_ref[d] for d in range(durables)]
+    first_d = as_float(dur_me == 0)
+    stay[0] = first_d + (1.0 - first_d) * stay[0]
+
+    def received(ref, kind, h, ag):
+        return ref[(h * ill_n + ag // ill_rows) * per_dest + kind * ill_rows + ag % ill_rows]
+
+    def interpolate(blocks, index, weight):
+        index = index.astype(jnp.int32)
+        low_block, low_lane = split_by(index, liq_rows)
+        high_block, high_lane = split_by(index + 1, liq_rows)
+        low = high = None
+        for h, block in enumerate(blocks):
+            low_h = jnp.take_along_axis(block, low_lane, axis=1, mode="promise_in_bounds")
+            high_h = jnp.take_along_axis(block, high_lane, axis=1, mode="promise_in_bounds")
+            low = low_h if h == 0 else jnp.where(low_block == h, low_h, low)
+            high = high_h if h == 0 else jnp.where(high_block == h, high_h, high)
+        return weight * low + (1.0 - weight) * high
+
+    def main_copy(i, step):
+        flip = lax.rem(i - ill_me + ill_n, ill_n)
+        return pltpu.make_async_remote_copy(
+            src_ref=value_two.at[pl.ds(i * grid_tiles, grid_tiles)],
+            dst_ref=values_in.at[pl.ds(ill_me * planes, grid_tiles), pl.ds(pl.multiple_of(liq_me * part, TILE), part)],
+            send_sem=value_send.at[i * liq_n + step], recv_sem=value_recv.at[flip * liq_n + step],
+            device_id={"liq": peer_of(liq_me, step, liq_n), "ill": i}, device_id_type=MESH_ID,
+        )
+
+    def plane_copy(i, step):
+        flip = lax.rem(i - ill_me + ill_n, ill_n)
+        return pltpu.make_async_remote_copy(
+            src_ref=value_two.at[pl.ds((i + 1) * grid_tiles, liq_n)],
+            dst_ref=values_in.at[
+                pl.ds(ill_me * planes + grid_tiles, liq_n), pl.ds(pl.multiple_of(liq_me * part, TILE), part)
+            ],
+            send_sem=plane_send.at[i * liq_n + step], recv_sem=plane_recv.at[flip * liq_n + step],
+            device_id={"liq": peer_of(liq_me, step, liq_n), "ill": i}, device_id_type=MESH_ID,
+        )
+
+    own_z = pl.ds(pl.multiple_of(liq_me * part, TILE), part)
+
+    def send_values(i):
+        for step in range(liq_n - 1, 0, -1):
+            main_copy(i, step).start()
+
+        @pl.when(ill_me != i)
+        def _():
+            main_copy(i, 0).start()
+
+        @pl.when(ill_me == i)
+        def _():
+            for k in range(grid_tiles):
+                values_in[i * planes + k, own_z, :] = value_two[i * grid_tiles + k]
+
+    def send_plane(i):
+        for step in range(liq_n - 1, 0, -1):
+            plane_copy(i, step).start()
+
+        @pl.when(ill_me != i)
+        def _():
+            plane_copy(i, 0).start()
+
+        @pl.when(ill_me == i)
+        def _():
+            for k in range(liq_n):
+                values_in[i * planes + grid_tiles + k, own_z, :] = value_two[(i + 1) * grid_tiles + k]
+
+    with scope("near"):
+        for flip in range(1, ill_n):
+            side_copy(flip).wait_recv()
+        for step, flip in peers:
+            near_copy(step, flip).wait_recv()
+
+    with scope("policy"):
+        for ag in range(ill_all):
+            i, a = divmod(ag, ill_rows)
+            own = jnp.broadcast_to(side_in[i, ill_rows, a : a + 1, :], (TILE, liq_rows))
+            for h in range(liq_n):
+                drifted = own * received(near_in, 0, h, ag) + (1.0 - own) * received(near_in, 0, h, min(ag + 1, ill_all - 1))
+                pencil_one[ag * liq_n + h] = lax.rsqrt(drifted)
+        for i in range(ill_n - 1, -1, -1):
+            for ag in range(i * ill_rows, (i + 1) * ill_rows):
+                blocks = [pencil_one[ag * liq_n + h] for h in range(liq_n)]
+                for h in range(liq_n):
+                    chosen = interpolate(blocks, received(near_in, 1, h, ag), received(near_in, 2, h, ag))
+                    value_two[ag * liq_n + h] = GROSS_RATE / (chosen * chosen)
+                    pencil_one[ill_all * liq_n + ag * liq_n + h] = chosen
+            send_values(i)
+            if i > 0:
+                send_plane(i - 1)
+
+    with scope("late"):
+        for step, flip in peers:
+            late_copy(step, flip).wait_recv()
+
+    lanes = 2 * liq_n
+    sub = iota((lanes, liq_rows), 0)
+    lane_at = iota((TILE, liq_rows), 1)
+    sub_block = jnp.where(sub < liq_n, sub, sub - liq_n).astype(f32)
+    lane_row = iota((liq_rows, liq_rows), 0).astype(f32).astype(jnp.bfloat16)
+    one = jnp.ones((liq_rows, liq_rows), jnp.bfloat16)
+    nil = jnp.zeros((liq_rows, liq_rows), jnp.bfloat16)
+
+    with scope("scatter"):
+        held = {}
+        for ag in range(ill_all):
+            for h in range(liq_n):
+                chosen = pencil_one[ill_all * liq_n + ag * liq_n + h]
+                share = jnp.clip(received(late_in, 0, h, ag) + SLOPE_GAIN * chosen, 0.0, 1.0)
+                mass = received(late_in, 1, h, ag)
+                target = received(late_in, 2, h, ag)
+                block = jnp.zeros(target.shape, f32)
+                for other in range(1, liq_n):
+                    block = block + jnp.where(target >= other * liq_rows, 1.0, 0.0)
+                held[ag, h] = (mass * share, mass * (1.0 - share), block, target - liq_rows * block)
+        for s in range(part):
+            totals = []
+            for ag in range(ill_all):
+                lefts, hots = [], []
+                for h in range(liq_n):
+                    low_t, high_t, hi_t, lo_t = (x[s : s + 1, :] for x in held[ag, h])
+                    both = jnp.where(sub < liq_n, low_t, high_t)
+                    both = jnp.where(hi_t == sub_block, both, 0.0)
+                    rounded = both.astype(jnp.bfloat16).astype(f32)
+                    lefts.append(jnp.concatenate([both, both - rounded], axis=0).astype(jnp.bfloat16))
+                    place = jnp.broadcast_to(lo_t, (2 * TILE, liq_rows)).astype(jnp.bfloat16)
+                    place = jnp.concatenate([place] * (liq_rows // (2 * TILE)), axis=0)
+                    hots.append(jnp.where(lane_row == place, one, nil))
+                found = lax.dot_general(
+                    jnp.concatenate(lefts, axis=1), jnp.concatenate(hots, axis=1), NT, preferred_element_type=f32
+                )
+                totals.append(found[:lanes] + found[lanes:])
+            to_row = [
+                jnp.broadcast_to(side_in[ag // ill_rows, ag % ill_rows, s : s + 1, :], (lanes, liq_rows))
+                for ag in range(ill_all)
+            ]
+            for dest in range(ill_all):
+                out = None
+                for ag in range(ill_all):
+                    here = jnp.where(to_row[ag] == dest, totals[ag], 0.0)
+                    out = here if out is None else out + here
+                placed[pl.ds(dest * part + s, lanes, stride=ill_all * part), :] = out
+
+    with scope("massout"):
+        for dest in range(ill_all):
+            carried = None
+            for h in range(liq_n):
+                low = placed[pl.ds((h * ill_all + dest) * part, part), :]
+                moved = pltpu.roll(placed[pl.ds(((liq_n + h) * ill_all + dest) * part, part), :], 1, 1)
+                total = low + jnp.where(lane_at > 0, moved, 0.0 if carried is None else carried)
+                carried = moved
+                mass_out[h * ill_all + dest] = total
+                depart_out[h * ill_all + dest] = (1.0 - stay[0]) * total
+
+    def mass_copy(step, flip):
+        there = at(step, flip)
+        return pltpu.make_async_remote_copy(
+            src_ref=mass_out.at[pl.ds(there["liq"] * ill_all + there["ill"] * ill_rows, ill_rows)],
+            dst_ref=mass_in.at[pl.ds(ill_me * ill_rows, ill_rows), own_z],
+            send_sem=mass_send.at[slot_of(step, flip)], recv_sem=mass_recv.at[slot_of(step, flip)],
+            device_id=there, device_id_type=MESH_ID,
+        )
+
+    def depart_copy(step, i):
+        liq_there = peer_of(liq_me, step, liq_n)
+        return pltpu.make_async_remote_copy(
+            src_ref=depart_out.at[pl.ds(liq_there * ill_all + i * ill_rows, ill_rows)],
+            dst_ref=mass_in.at[pl.ds(group, ill_rows), own_z],
+            send_sem=depart_send.at[step * ill_n + i], recv_sem=depart_recv.at[step],
+            device_id={"dur": jnp.maximum(dur_me - 1, 0), "liq": liq_there, "ill": i}, device_id_type=MESH_ID,
+        )
+
+    departs = (dur_me > 0) & (ill_me == 0)
+
+    @pl.when(departs)
+    def _():
+        pl.semaphore_wait(ready_sem, 1)
+        for step in range(liq_n - 1, -1, -1):
+            for i in range(ill_n):
+                depart_copy(step, i).start()
+
+    for step, flip in peers:
+        mass_copy(step, flip).start()
+    for a in range(ill_rows):
+        mass_in[ill_me * ill_rows + a, own_z, :] = mass_out[liq_me * ill_all + ill_me * ill_rows + a]
+
+    with scope("values"):
+        for step, flip in peers:
+            pltpu.make_async_remote_copy(
+                src_ref=value_two.at[pl.ds(0, grid_tiles)],
+                dst_ref=values_in.at[pl.ds(0, grid_tiles), pl.ds(0, part)],
+                send_sem=value_send.at[0], recv_sem=value_recv.at[slot_of(step, flip)],
+                device_id=at(step, flip), device_id_type=MESH_ID,
+            ).wait_recv()
+
+        @pl.when(ill_me < ill_n - 1)
+        def _():
+            for step, flip in peers:
+                pltpu.make_async_remote_copy(
+                    src_ref=value_two.at[pl.ds(0, liq_n)],
+                    dst_ref=values_in.at[pl.ds(0, liq_n), pl.ds(0, part)],
+                    send_sem=plane_send.at[0], recv_sem=plane_recv.at[slot_of(step, flip)],
+                    device_id=at(step, flip), device_id_type=MESH_ID,
+                ).wait_recv()
+
+    with scope("second"):
+        is_last = ill_me == ill_n - 1
+        for d in range(durables):
+            expected = []
+            for a in range(ill_rows + 1):
+                wide = jnp.concatenate([values_in[d * planes + a * liq_n + h] for h in range(liq_n)], axis=1)
+                expected.append(times(left_two, wide))
+            expected[ill_rows] = jnp.where(is_last, expected[ill_rows - 1], expected[ill_rows])
+            for a in range(ill_rows):
+                own = drift_ref[a]
+                found = lax.rsqrt(own * expected[a] + (1.0 - own) * expected[a + 1])
+                for h in range(liq_n):
+                    pencil_two[(d * ill_rows + a) * liq_n + h] = found[:, h * liq_rows : (h + 1) * liq_rows]
+        for k, (d, a) in enumerate(kinds):
+            for q in range(liq_n):
+                base = (d * liq_n + q) * per_dest
+                blocks = [pencil_two[k * liq_n + h, pl.ds(q * part, part), :] for h in range(liq_n)]
+                consumption_ref[rows_at(d, a, q), :] = interpolate(
+                    blocks, near_out[base + ill_rows + a], near_out[base + 2 * ill_rows + a]
+                )
+
+    with scope("mass"):
+        for step, flip in peers:
+            mass_copy(step, flip).wait_recv()
+
+        @pl.when(dur_me < dur_n - 1)
+        def _():
+            for step in range(liq_n):
+                depart_copy(step, 0).wait_recv()
+
+    with scope("next"):
+        settled = []
+        for d, a in kinds:
+            after = mass_in[(d + 1) * ill_rows + a]
+            if d + 1 < durables:
+                after = (1.0 - stay[d + 1]) * after
+            settled.append(stay[d] * mass_in[d * ill_rows + a] + after)
+        high, low = halves_of(transition)
+        found = lax.dot_general(
+            jnp.concatenate([high, high, low], axis=0), stack_data(jnp.concatenate(settled, axis=1)),
+            (((0,), (0,)), ((), ())), preferred_element_type=f32,
+        )
+        for k, (d, a) in enumerate(kinds):
+            for q in range(liq_n):
+                next_ref[rows_at(d, a, q), :] = found[q * part : (q + 1) * part, k * liq_rows : (k + 1) * liq_rows]
+
+    for flip in range(1, ill_n):
+        side_copy(flip).wait_send()
+    for step, flip in peers:
+        near_copy(step, flip).wait_send()
+        late_copy(step, flip).wait_send()
+        mass_copy(step, flip).wait_send()
+
+    for i in range(ill_n):
+        for step in range(1, liq_n):
+            main_copy(i, step).wait_send()
+            if i < ill_n - 1:
+                plane_copy(i, step).wait_send()
+
+        @pl.when(ill_me != i)
+        def _():
+            main_copy(i, 0).wait_send()
+            if i < ill_n - 1:
+                plane_copy(i, 0).wait_send()
+
+    @pl.when(departs)
+    def _():
+        for step in range(liq_n):
+            for i in range(ill_n):
+                depart_copy(step, i).wait_send()
+
+
 def store(consumption_ref, next_ref, consumption_hbm, next_hbm, sem):
     copies = [
         pltpu.make_async_copy(consumption_ref, consumption_hbm, sem.at[0]),
@@ -418,6 +887,107 @@
         copy.start()
     for copy in copies:
         copy.wait()
+
+
+def window_scratch(dims):
+    incomes, durables, ill_rows, liq_rows, liq_n, ill_n, dur_n = dims
+    f32 = jnp.float32
+    rows, plane_rows = incomes * durables * ill_rows, incomes * ill_rows
+    block = (rows, liq_rows)
+    dma = pltpu.SemaphoreType.DMA
+    return [
+        pltpu.VMEM(block, f32),
+        pltpu.VMEM((incomes, incomes), f32),
+        pltpu.VMEM((1, incomes), f32),
+        pltpu.VMEM(block, jnp.int32),
+        pltpu.VMEM(block, f32),
+        pltpu.VMEM(block, f32),
+        pltpu.VMEM(block, f32),
+        pltpu.VMEM(block, jnp.int32),
+        pltpu.VMEM(block, f32),
+        pltpu.SMEM((ill_rows,), f32),
+        pltpu.SMEM((durables,), f32),
+        pltpu.SMEM((durables * ill_rows, incomes), jnp.int32),
+        dma((12,)),
+        pltpu.VMEM((rows, rows), f32),
+        pltpu.VMEM((rows, rows), f32),
+        pltpu.VMEM((rows, rows), f32),
+        pltpu.VMEM((rows, rows), f32),
+        pltpu.VMEM((rows, rows), f32),
+        pltpu.VMEM((rows, plane_rows), f32),
+        pltpu.VMEM((2,) + block, f32),
+        pltpu.VMEM(block, f32),
+        pltpu.VMEM((2 * liq_n,) + block, f32),
+        pltpu.VMEM(block, f32),
+        pltpu.VMEM(block, f32),
+        pltpu.VMEM(block, jnp.int32),
+        pltpu.VMEM(block, f32),
+        pltpu.VMEM((2 * ill_n * liq_n * plane_rows, liq_rows), f32),
+        pltpu.VMEM((ill_n * liq_n * rows, liq_rows), f32),
+        pltpu.VMEM((durables * (ill_n - 1), liq_n * plane_rows, liq_rows), f32),
+        pltpu.VMEM((durables * liq_n, plane_rows, liq_rows), f32),
+        pltpu.VMEM((durables * (liq_n - 1), plane_rows, liq_rows), f32),
+        pltpu.VMEM(block, f32),
+        pltpu.VMEM((plane_rows, liq_rows), f32),
+        pltpu.VMEM((plane_rows, liq_rows), f32),
+        dma((2,)),
+        dma((2,)),
+        dma((4 * liq_n,)),
+        dma((4 * liq_n,)),
+        dma((durables * (ill_n - 1),)),
+        dma((durables * (ill_n - 1),)),
+        dma((durables * (liq_n - 1),)),
+        dma((durables * (liq_n - 1),)),
+        dma((1,)),
+        dma((1,)),
+    ]
+
+
+def transposed_scratch(dims):
+    incomes, durables, ill_rows, liq_rows, liq_n, ill_n, dur_n = dims
+    f32 = jnp.float32
+    block = (incomes * durables * ill_rows, liq_rows)
+    dma = pltpu.SemaphoreType.DMA
+    part = incomes // liq_n
+    ill_all = ill_n * ill_rows
+    tiles = lambda n: pltpu.VMEM((n, part, liq_rows), f32)
+    slabs = lambda n: pltpu.VMEM((n, incomes, liq_rows), f32)
+    bundle = durables * liq_n * 3 * ill_rows
+    peers = liq_n * ill_n
+    return [
+        pltpu.VMEM(block, f32),
+        pltpu.VMEM((incomes, incomes), f32),
+        pltpu.VMEM((1, incomes), f32),
+        pltpu.VMEM(block, jnp.int32),
+        pltpu.VMEM(block, f32),
+        pltpu.VMEM(block, f32),
+        pltpu.VMEM(block, f32),
+        pltpu.VMEM(block, jnp.int32),
+        pltpu.VMEM(block, f32),
+        pltpu.VMEM((durables * ill_rows, incomes), jnp.int32),
+        pltpu.SMEM((ill_rows,), f32),
+        pltpu.SMEM((durables,), f32),
+        dma((12,)),
+        tiles(bundle),
+        tiles(bundle),
+        tiles(bundle),
+        tiles(bundle),
+        pltpu.VMEM((durables, ill_rows + 1, TILE, liq_rows), f32),
+        pltpu.VMEM((ill_n, ill_rows + 1, TILE, liq_rows), f32),
+        tiles(2 * ill_all * liq_n),
+        tiles(ill_all * liq_n),
+        slabs(durables * (ill_rows + 1) * liq_n),
+        slabs(durables * ill_rows * liq_n),
+        pltpu.VMEM((2 * liq_n * ill_all * part, liq_rows), f32),
+        tiles(liq_n * ill_all),
+        tiles(liq_n * ill_all),
+        slabs((durables + 1) * ill_rows),
+    ] + [
+        dma((n,))
+        for n in (
+            peers, peers, peers, peers, ill_n, ill_n, peers, peers, peers, peers, peers, peers, peers, liq_n,
+        )
+    ] + [pltpu.SemaphoreType.REGULAR]
 
 
 def body(
@@ -438,7 +1008,6 @@
     incomes, durables, ill_rows, liq_rows = shape
     liq_n, ill_n, dur_n = (lax.axis_size(name) for name in ("liq", "ill", "dur"))
     rows = incomes * durables * ill_rows
-    plane_rows = incomes * ill_rows
     flat = lambda x: x.reshape(rows, liq_rows)
     anywhere = pl.BlockSpec(memory_space=pl.ANY)
     f32 = jnp.float32
@@ -448,59 +1017,21 @@
     held = pltpu.VMEM(block, f32)
     result = jax.ShapeDtypeStruct(block, f32)
     dims = (incomes, durables, ill_rows, liq_rows, liq_n, ill_n, dur_n)
+    transposed = (
+        ill_n == 2 and durables == ill_n and liq_n * 2 == TILE and incomes == liq_n * TILE and ill_rows < TILE
+    )
+    if transposed:
+        step_kernel, scratch, name = transposed_kernel, transposed_scratch(dims), "transposed_window"
+    else:
+        step_kernel, scratch, name = kernel, window_scratch(dims), "window"
     outs = pl.pallas_call(
-        functools.partial(kernel, dims),
+        functools.partial(step_kernel, dims),
         out_shape=(held, held),
         in_specs=[anywhere] * 12,
         out_specs=(vmem, vmem),
-        scratch_shapes=[
-            pltpu.VMEM(block, f32),
-            pltpu.VMEM((incomes, incomes), f32),
-            pltpu.VMEM((1, incomes), f32),
-            pltpu.VMEM(block, jnp.int32),
-            pltpu.VMEM(block, f32),
-            pltpu.VMEM(block, f32),
-            pltpu.VMEM(block, f32),
-            pltpu.VMEM(block, jnp.int32),
-            pltpu.VMEM(block, f32),
-            pltpu.SMEM((ill_rows,), f32),
-            pltpu.SMEM((durables,), f32),
-            pltpu.SMEM((durables * ill_rows, incomes), jnp.int32),
-            dma((12,)),
-            pltpu.VMEM((rows, rows), f32),
-            pltpu.VMEM((rows, rows), f32),
-            pltpu.VMEM((rows, rows), f32),
-            pltpu.VMEM((rows, rows), f32),
-            pltpu.VMEM((rows, rows), f32),
-            pltpu.VMEM((rows, plane_rows), f32),
-            pltpu.VMEM((2,) + block, f32),
-            pltpu.VMEM(block, f32),
-            pltpu.VMEM((2 * liq_n,) + block, f32),
-            pltpu.VMEM(block, f32),
-            pltpu.VMEM(block, f32),
-            pltpu.VMEM(block, jnp.int32),
-            pltpu.VMEM(block, f32),
-            pltpu.VMEM((2 * ill_n * liq_n * plane_rows, liq_rows), f32),
-            pltpu.VMEM((ill_n * liq_n * rows, liq_rows), f32),
-            pltpu.VMEM((durables * (ill_n - 1), liq_n * plane_rows, liq_rows), f32),
-            pltpu.VMEM((durables * liq_n, plane_rows, liq_rows), f32),
-            pltpu.VMEM((durables * (liq_n - 1), plane_rows, liq_rows), f32),
-            pltpu.VMEM(block, f32),
-            pltpu.VMEM((plane_rows, liq_rows), f32),
-            pltpu.VMEM((plane_rows, liq_rows), f32),
-            dma((2,)),
-            dma((2,)),
-            dma((4 * liq_n,)),
-            dma((4 * liq_n,)),
-            dma((durables * (ill_n - 1),)),
-            dma((durables * (ill_n - 1),)),
-            dma((durables * (liq_n - 1),)),
-            dma((durables * (liq_n - 1),)),
-            dma((1,)),
-            dma((1,)),
-        ],
+        scratch_shapes=scratch,
         compiler_params=pltpu.CompilerParams(collective_id=0, has_side_effects=True),
-        name="window",
+        name=name,
     )(
         flat(marginal_value),
         transition,

time: 22.1 us -> 18.2 us (0.82)
  Pallas kernels: 21.2 us -> 17.3 us
    pallas_call x1, Pallas kernels: 20.5 us -> 16.6 us  [body(): pl.pallas_call(functools.partial(step_kernel, dims), out_shape=(held, hel...]
where the time goes in v1:
time: 18.2 us; the launch traced here: 17.9 us
  Pallas kernels  17.3 us (95%)
  between operations  0.64 us (4%)
    pallas_call x1, Pallas kernels, body(): pl.pallas_call(functools.partial(step_kernel, dims), out_shape=(held, hel...  16.6 us
    pallas_call x1, Pallas kernels, body(): pl.pallas_call(store, out_shape=(result, result), in_specs=[vmem, vmem],...  0.67 us

profile of v1, /device:TPU:0, one launch (start us, length us, event | category | flops | bytes accessed | tf_op | source)
XLA Modules:
  0.0 17.9 jit_solution(8359683293652436393)
XLA Ops:
  0.6 16.6 %transposed_window.1 = (f32[128,128]{1,0:T(8,128)S(1)}, f32[128,128]{1,0:T(8,128)S(1)}) custom-call(f32[128,128]{1,0:T(8,128)} %bitcast.13, f32[32,32]{1,0:T(8,128)} %transition_hbm.1, f32[1,32]{1,0:T(1,128)} %bitcast.21, f32[2]{0:T(128)} %drift_hbm.1, f32[2]{0:T(128)} %keep_hbm.1, s32[128,128]{1,0:T(8,128)} %bitcast.14, f32[128,128]{1,0:T(8,128)} %bitcast.15, ...), custom_call_target="tpu_custom_call" | custom-call | tf_op jit(solution)/shard_map/transposed_window/pallas_call | solution.py:1027
  17.3 0.7 %store.1 = (f32[128,128]{1,0:T(8,128)}, f32[128,128]{1,0:T(8,128)}) custom-call(f32[128,128]{1,0:T(8,128)S(1)} %get-tuple-element.6.consumption_ref, f32[128,128]{1,0:T(8,128)S(1)} %get-tuple-element.7.next_ref), custom_call_target="tpu_custom_call" | custom-call | tf_op jit(solution)/shard_map/store/pallas_call | solution.py:1049

commit v2 on v1

--- a/solution.py
+++ b/solution.py
@@ -431,28 +431,24 @@
     consumption_ref, next_ref,
     value_ref, transition_ref, shock_ref, index_ref, weight_ref, steady_ref, lottery_ref, target_ref,
     population_ref, ill_target_ref, drift_ref, keep_ref, load_sem,
-    near_out, near_in, late_out, late_in, side_out, side_in,
-    pencil_one, value_two, values_in, pencil_two, placed, mass_out, depart_out, mass_in,
-    near_send, near_recv, late_send, late_recv, side_send, side_recv,
-    value_send, value_recv, plane_send, plane_recv, mass_send, mass_recv, depart_send, depart_recv, ready_sem,
+    near_out, near_in, late_out, late_in, side_out, side_in, pair_in,
+    pencil_one, value_two, values_in, pencil_two, found_out, found_in, placed, mass_out, depart_out, mass_in,
+    near_send, near_recv, late_send, late_recv, side_send, side_recv, pair_send, pair_recv,
+    value_send, value_recv, found_send, found_recv, mass_send, mass_recv, depart_send, depart_recv, ready_sem,
 ):
     incomes, durables, ill_rows, liq_rows, liq_n, ill_n, dur_n = dims
     group = durables * ill_rows
     ill_all = ill_n * ill_rows
     part = incomes // liq_n
     per_dest = 3 * ill_rows
-    grid_tiles = ill_rows * liq_n
-    planes = (ill_rows + 1) * liq_n
     constant = jnp.float32(DISCOUNT * GROSS_RATE)
     f32 = jnp.float32
     liq_me, ill_me, dur_me = (lax.axis_index(name) for name in ("liq", "ill", "dur"))
+    far_first = range(liq_n - 1, 0, -1)
     peers = [(step, flip) for step in range(liq_n - 1, -1, -1) for flip in range(ill_n) if step or flip]
 
     def at(step, flip):
         return {"liq": peer_of(liq_me, step, liq_n), "ill": peer_of(ill_me, flip, ill_n)}
-
-    def slot_of(step, flip):
-        return flip * liq_n + step
 
     barrier = pltpu.get_barrier_semaphore()
     for step, flip in peers:
@@ -507,10 +503,9 @@
         load.wait()
     for k, (d, a) in enumerate(kinds):
         for q in range(liq_n):
-            base = (d * liq_n + q) * per_dest
-            near_out[base + a] = wide[q * part : (q + 1) * part, k * liq_rows : (k + 1) * liq_rows]
-            near_out[base + ill_rows + a] = index_ref[rows_at(d, a, q), :].astype(f32)
-            near_out[base + 2 * ill_rows + a] = weight_ref[rows_at(d, a, q), :]
+            near_out[d * liq_n + q, a] = wide[q * part : (q + 1) * part, k * liq_rows : (k + 1) * liq_rows]
+            near_out[d * liq_n + q, ill_rows + a] = index_ref[rows_at(d, a, q), :].astype(f32)
+            near_out[d * liq_n + q, 2 * ill_rows + a] = weight_ref[rows_at(d, a, q), :]
 
     for load in loads[5:7]:
         load.wait()
@@ -546,11 +541,22 @@
     def bundle_copy(out_ref, in_ref, send, recv, step, flip):
         there = at(step, flip)
         return pltpu.make_async_remote_copy(
-            src_ref=out_ref.at[pl.ds((there["ill"] * liq_n + there["liq"]) * per_dest, per_dest)],
-            dst_ref=in_ref.at[pl.ds((liq_me * ill_n + ill_me) * per_dest, per_dest)],
-            send_sem=send.at[slot_of(step, flip)], recv_sem=recv.at[slot_of(step, flip)],
-            device_id=there, device_id_type=MESH_ID,
-        )
+            src_ref=out_ref.at[there["ill"] * liq_n + there["liq"]], dst_ref=in_ref.at[liq_me * ill_n + ill_me],
+            send_sem=send.at[0], recv_sem=recv.at[0], device_id=there, device_id_type=MESH_ID,
+        )
+
+    def bundle_all(out_ref, in_ref, send, recv):
+        span = pl.ds(0, len(peers))
+        return pltpu.make_async_remote_copy(
+            src_ref=out_ref.at[span], dst_ref=in_ref.at[span], send_sem=send.at[0], recv_sem=recv.at[0],
+            device_id=at(0, 1), device_id_type=MESH_ID,
+        )
+
+    def near_all():
+        return bundle_all(near_out, near_in, near_send, near_recv)
+
+    def late_all():
+        return bundle_all(late_out, late_in, late_send, late_recv)
 
     def near_copy(step, flip):
         return bundle_copy(near_out, near_in, near_send, near_recv, step, flip)
@@ -562,7 +568,15 @@
         there = at(0, flip)
         return pltpu.make_async_remote_copy(
             src_ref=side_out.at[there["ill"]], dst_ref=side_in.at[ill_me],
-            send_sem=side_send.at[flip], recv_sem=side_recv.at[flip], device_id=there, device_id_type=MESH_ID,
+            send_sem=side_send.at[flip - 1], recv_sem=side_recv.at[flip - 1], device_id=there, device_id_type=MESH_ID,
+        )
+
+    def pair_copy(flip):
+        there = at(0, flip)
+        return pltpu.make_async_remote_copy(
+            src_ref=near_out.at[pl.ds(there["ill"] * liq_n, liq_n), pl.ds(ill_rows, 2 * ill_rows)],
+            dst_ref=pair_in.at[ill_me], send_sem=pair_send.at[flip - 1], recv_sem=pair_recv.at[flip - 1],
+            device_id=there, device_id_type=MESH_ID,
         )
 
     for step, flip in peers:
@@ -574,27 +588,25 @@
         load.wait()
     for d, a in kinds:
         for q in range(liq_n):
-            base = (d * liq_n + q) * per_dest
             span = rows_at(d, a, q)
-            late_out[base + a] = lottery_ref[span, :] - SLOPE_GAIN * steady_ref[span, :]
-            late_out[base + ill_rows + a] = population_ref[span, :]
-            late_out[base + 2 * ill_rows + a] = target_ref[span, :].astype(f32)
+            late_out[d * liq_n + q, a] = lottery_ref[span, :] - SLOPE_GAIN * steady_ref[span, :]
+            late_out[d * liq_n + q, ill_rows + a] = population_ref[span, :]
+            late_out[d * liq_n + q, 2 * ill_rows + a] = target_ref[span, :].astype(f32)
     for step, flip in peers:
         late_copy(step, flip).start()
-
-    own_out = (ill_me * liq_n + liq_me) * per_dest
-    own_in = (liq_me * ill_n + ill_me) * per_dest
+    for flip in range(1, ill_n):
+        pair_copy(flip).start()
+
+    own_out = ill_me * liq_n + liq_me
+    own_in = liq_me * ill_n + ill_me
     for k in range(per_dest):
-        near_in[own_in + k] = near_out[own_out + k]
-        late_in[own_in + k] = late_out[own_out + k]
+        near_in[own_in, k] = near_out[own_out, k]
+        late_in[own_in, k] = late_out[own_out, k]
     for k in range(ill_rows + 1):
         side_in[ill_me, k] = side_out[ill_me, k]
-
-    @pl.when(ill_me == ill_n - 1)
-    def _():
-        for d in range(durables):
-            for h in range(liq_n):
-                values_in[d * planes + grid_tiles + h] = jnp.zeros((incomes, liq_rows), f32)
+    for q in range(liq_n):
+        for k in range(2 * ill_rows):
+            pair_in[ill_me, q, k] = near_out[ill_me * liq_n + q, ill_rows + k]
 
     @pl.when(dur_me == dur_n - 1)
     def _():
@@ -606,7 +618,7 @@
     stay[0] = first_d + (1.0 - first_d) * stay[0]
 
     def received(ref, kind, h, ag):
-        return ref[(h * ill_n + ag // ill_rows) * per_dest + kind * ill_rows + ag % ill_rows]
+        return ref[h * ill_n + ag // ill_rows, kind * ill_rows + ag % ill_rows]
 
     def interpolate(blocks, index, weight):
         index = index.astype(jnp.int32)
@@ -620,59 +632,28 @@
             high = high_h if h == 0 else jnp.where(high_block == h, high_h, high)
         return weight * low + (1.0 - weight) * high
 
-    def main_copy(i, step):
-        flip = lax.rem(i - ill_me + ill_n, ill_n)
-        return pltpu.make_async_remote_copy(
-            src_ref=value_two.at[pl.ds(i * grid_tiles, grid_tiles)],
-            dst_ref=values_in.at[pl.ds(ill_me * planes, grid_tiles), pl.ds(pl.multiple_of(liq_me * part, TILE), part)],
-            send_sem=value_send.at[i * liq_n + step], recv_sem=value_recv.at[flip * liq_n + step],
-            device_id={"liq": peer_of(liq_me, step, liq_n), "ill": i}, device_id_type=MESH_ID,
-        )
-
-    def plane_copy(i, step):
-        flip = lax.rem(i - ill_me + ill_n, ill_n)
-        return pltpu.make_async_remote_copy(
-            src_ref=value_two.at[pl.ds((i + 1) * grid_tiles, liq_n)],
-            dst_ref=values_in.at[
-                pl.ds(ill_me * planes + grid_tiles, liq_n), pl.ds(pl.multiple_of(liq_me * part, TILE), part)
-            ],
-            send_sem=plane_send.at[i * liq_n + step], recv_sem=plane_recv.at[flip * liq_n + step],
-            device_id={"liq": peer_of(liq_me, step, liq_n), "ill": i}, device_id_type=MESH_ID,
-        )
-
     own_z = pl.ds(pl.multiple_of(liq_me * part, TILE), part)
 
-    def send_values(i):
-        for step in range(liq_n - 1, 0, -1):
-            main_copy(i, step).start()
-
-        @pl.when(ill_me != i)
-        def _():
-            main_copy(i, 0).start()
-
-        @pl.when(ill_me == i)
-        def _():
-            for k in range(grid_tiles):
-                values_in[i * planes + k, own_z, :] = value_two[i * grid_tiles + k]
-
-    def send_plane(i):
-        for step in range(liq_n - 1, 0, -1):
-            plane_copy(i, step).start()
-
-        @pl.when(ill_me != i)
-        def _():
-            plane_copy(i, 0).start()
-
-        @pl.when(ill_me == i)
-        def _():
-            for k in range(liq_n):
-                values_in[i * planes + grid_tiles + k, own_z, :] = value_two[(i + 1) * grid_tiles + k]
+    chunk = ill_rows * liq_n
+
+    def value_copy(i, step):
+        span = pl.ds(i * chunk, chunk)
+        return pltpu.make_async_remote_copy(
+            src_ref=value_two.at[span], dst_ref=values_in.at[span, own_z], send_sem=value_send.at[0],
+            recv_sem=value_recv.at[0], device_id={"liq": peer_of(liq_me, step, liq_n)}, device_id_type=MESH_ID,
+        )
+
+    def value_all():
+        span = pl.ds(0, (liq_n - 1) * ill_all)
+        return pltpu.make_async_remote_copy(
+            src_ref=values_in.at[span], dst_ref=values_in.at[span], send_sem=value_send.at[0],
+            recv_sem=value_recv.at[0], device_id=at(1, 0), device_id_type=MESH_ID,
+        )
 
     with scope("near"):
         for flip in range(1, ill_n):
             side_copy(flip).wait_recv()
-        for step, flip in peers:
-            near_copy(step, flip).wait_recv()
+        near_all().wait_recv()
 
     with scope("policy"):
         for ag in range(ill_all):
@@ -681,20 +662,17 @@
             for h in range(liq_n):
                 drifted = own * received(near_in, 0, h, ag) + (1.0 - own) * received(near_in, 0, h, min(ag + 1, ill_all - 1))
                 pencil_one[ag * liq_n + h] = lax.rsqrt(drifted)
-        for i in range(ill_n - 1, -1, -1):
-            for ag in range(i * ill_rows, (i + 1) * ill_rows):
-                blocks = [pencil_one[ag * liq_n + h] for h in range(liq_n)]
-                for h in range(liq_n):
-                    chosen = interpolate(blocks, received(near_in, 1, h, ag), received(near_in, 2, h, ag))
-                    value_two[ag * liq_n + h] = GROSS_RATE / (chosen * chosen)
-                    pencil_one[ill_all * liq_n + ag * liq_n + h] = chosen
-            send_values(i)
-            if i > 0:
-                send_plane(i - 1)
-
-    with scope("late"):
-        for step, flip in peers:
-            late_copy(step, flip).wait_recv()
+        for ag in range(ill_all):
+            blocks = [pencil_one[ag * liq_n + h] for h in range(liq_n)]
+            for h in range(liq_n):
+                chosen = interpolate(blocks, received(near_in, 1, h, ag), received(near_in, 2, h, ag))
+                found = GROSS_RATE / (chosen * chosen)
+                value_two[ag * liq_n + h] = found
+                values_in[ag * liq_n + h, own_z, :] = found
+                pencil_one[ill_all * liq_n + ag * liq_n + h] = chosen
+            if ag % ill_rows == ill_rows - 1:
+                for step in far_first:
+                    value_copy(ag // ill_rows, step).start()
 
     lanes = 2 * liq_n
     sub = iota((lanes, liq_rows), 0)
@@ -704,10 +682,11 @@
     one = jnp.ones((liq_rows, liq_rows), jnp.bfloat16)
     nil = jnp.zeros((liq_rows, liq_rows), jnp.bfloat16)
 
-    with scope("scatter"):
+    def scattered(steps):
         held = {}
         for ag in range(ill_all):
-            for h in range(liq_n):
+            for step in steps:
+                h = step
                 chosen = pencil_one[ill_all * liq_n + ag * liq_n + h]
                 share = jnp.clip(received(late_in, 0, h, ag) + SLOPE_GAIN * chosen, 0.0, 1.0)
                 mass = received(late_in, 1, h, ag)
@@ -715,13 +694,12 @@
                 block = jnp.zeros(target.shape, f32)
                 for other in range(1, liq_n):
                     block = block + jnp.where(target >= other * liq_rows, 1.0, 0.0)
-                held[ag, h] = (mass * share, mass * (1.0 - share), block, target - liq_rows * block)
+                held[ag, step] = (mass * share, mass * (1.0 - share), block, target - liq_rows * block)
         for s in range(part):
-            totals = []
             for ag in range(ill_all):
                 lefts, hots = [], []
-                for h in range(liq_n):
-                    low_t, high_t, hi_t, lo_t = (x[s : s + 1, :] for x in held[ag, h])
+                for step in steps:
+                    low_t, high_t, hi_t, lo_t = (x[s : s + 1, :] for x in held[ag, step])
                     both = jnp.where(sub < liq_n, low_t, high_t)
                     both = jnp.where(hi_t == sub_block, both, 0.0)
                     rounded = both.astype(jnp.bfloat16).astype(f32)
@@ -732,17 +710,26 @@
                 found = lax.dot_general(
                     jnp.concatenate(lefts, axis=1), jnp.concatenate(hots, axis=1), NT, preferred_element_type=f32
                 )
-                totals.append(found[:lanes] + found[lanes:])
-            to_row = [
-                jnp.broadcast_to(side_in[ag // ill_rows, ag % ill_rows, s : s + 1, :], (lanes, liq_rows))
-                for ag in range(ill_all)
-            ]
-            for dest in range(ill_all):
-                out = None
-                for ag in range(ill_all):
-                    here = jnp.where(to_row[ag] == dest, totals[ag], 0.0)
-                    out = here if out is None else out + here
-                placed[pl.ds(dest * part + s, lanes, stride=ill_all * part), :] = out
+                yield s, ag, found[:lanes] + found[lanes:]
+
+    with scope("late"):
+        late_all().wait_recv()
+    with scope("scatter"):
+        totals = []
+        for s, ag, total in scattered(range(liq_n)):
+            totals.append(total)
+            if ag == ill_all - 1:
+                to_row = [
+                    jnp.broadcast_to(side_in[k // ill_rows, k % ill_rows, s : s + 1, :], (lanes, liq_rows))
+                    for k in range(ill_all)
+                ]
+                for dest in range(ill_all):
+                    out = None
+                    for k in range(ill_all):
+                        here = jnp.where(to_row[k] == dest, totals[k], 0.0)
+                        out = here if out is None else out + here
+                    placed[pl.ds(dest * part + s, lanes, stride=ill_all * part), :] = out
+                totals = []
 
     with scope("massout"):
         for dest in range(ill_all):
@@ -760,8 +747,21 @@
         return pltpu.make_async_remote_copy(
             src_ref=mass_out.at[pl.ds(there["liq"] * ill_all + there["ill"] * ill_rows, ill_rows)],
             dst_ref=mass_in.at[pl.ds(ill_me * ill_rows, ill_rows), own_z],
-            send_sem=mass_send.at[slot_of(step, flip)], recv_sem=mass_recv.at[slot_of(step, flip)],
-            device_id=there, device_id_type=MESH_ID,
+            send_sem=mass_send.at[0], recv_sem=mass_recv.at[0], device_id=there, device_id_type=MESH_ID,
+        )
+
+    def mass_all():
+        span = pl.ds(0, len(peers) * ill_rows)
+        return pltpu.make_async_remote_copy(
+            src_ref=mass_out.at[span], dst_ref=mass_out.at[span], send_sem=mass_send.at[0],
+            recv_sem=mass_recv.at[0], device_id=at(0, 1), device_id_type=MESH_ID,
+        )
+
+    def depart_all(count):
+        span = pl.ds(0, count * ill_rows)
+        return pltpu.make_async_remote_copy(
+            src_ref=depart_out.at[span], dst_ref=depart_out.at[span], send_sem=depart_send.at[0],
+            recv_sem=depart_recv.at[0], device_id=at(0, 1), device_id_type=MESH_ID,
         )
 
     def depart_copy(step, i):
@@ -769,7 +769,7 @@
         return pltpu.make_async_remote_copy(
             src_ref=depart_out.at[pl.ds(liq_there * ill_all + i * ill_rows, ill_rows)],
             dst_ref=mass_in.at[pl.ds(group, ill_rows), own_z],
-            send_sem=depart_send.at[step * ill_n + i], recv_sem=depart_recv.at[step],
+            send_sem=depart_send.at[0], recv_sem=depart_recv.at[0],
             device_id={"dur": jnp.maximum(dur_me - 1, 0), "liq": liq_there, "ill": i}, device_id_type=MESH_ID,
         )
 
@@ -787,54 +787,71 @@
     for a in range(ill_rows):
         mass_in[ill_me * ill_rows + a, own_z, :] = mass_out[liq_me * ill_all + ill_me * ill_rows + a]
 
+    def found_copy(flip):
+        there = at(0, flip)
+        return pltpu.make_async_remote_copy(
+            src_ref=found_out.at[flip - 1], dst_ref=found_in.at[flip - 1],
+            send_sem=found_send.at[flip - 1], recv_sem=found_recv.at[flip - 1], device_id=there, device_id_type=MESH_ID,
+        )
+
+    for flip in range(1, ill_n):
+        side_copy(flip).wait_send()
+        pair_copy(flip).wait_send()
+        pair_copy(flip).wait_recv()
+    near_all().wait_send()
+    late_all().wait_send()
     with scope("values"):
-        for step, flip in peers:
-            pltpu.make_async_remote_copy(
-                src_ref=value_two.at[pl.ds(0, grid_tiles)],
-                dst_ref=values_in.at[pl.ds(0, grid_tiles), pl.ds(0, part)],
-                send_sem=value_send.at[0], recv_sem=value_recv.at[slot_of(step, flip)],
-                device_id=at(step, flip), device_id_type=MESH_ID,
-            ).wait_recv()
-
-        @pl.when(ill_me < ill_n - 1)
+        value_all().wait_recv()
+
+    with scope("second"):
+        expected = []
+        for ag in range(ill_all):
+            wide = jnp.concatenate([values_in[ag * liq_n + h] for h in range(liq_n)], axis=1)
+            expected.append(times(left_two, wide))
+        for ag in range(ill_all):
+            i, a = divmod(ag, ill_rows)
+            own = jnp.broadcast_to(side_in[i, ill_rows, a : a + 1, :], (incomes, liq_rows))
+            own = jnp.concatenate([own] * liq_n, axis=1)
+            found = lax.rsqrt(own * expected[ag] + (1.0 - own) * expected[min(ag + 1, ill_all - 1)])
+            for h in range(liq_n):
+                pencil_two[ag * liq_n + h] = found[:, h * liq_rows : (h + 1) * liq_rows]
+        for flip in range(ill_n - 1, -1, -1):
+            i = peer_of(ill_me, flip, ill_n)
+            for a in range(ill_rows):
+                for q in range(liq_n):
+                    blocks = [
+                        pencil_two[(i * ill_rows + a) * liq_n + h, pl.ds(q * part, part), :] for h in range(liq_n)
+                    ]
+                    found = interpolate(blocks, pair_in[i, q, a], pair_in[i, q, ill_rows + a])
+                    if flip:
+                        found_out[flip - 1, q * ill_rows + a] = found
+                    else:
+                        consumption_ref[rows_at(ill_me, a, q), :] = found
+            if flip:
+                found_copy(flip).start()
+
+    with scope("sends"):
+        value_all().wait_send()
+        mass_all().wait_send()
+
+        @pl.when(departs)
         def _():
-            for step, flip in peers:
-                pltpu.make_async_remote_copy(
-                    src_ref=value_two.at[pl.ds(0, liq_n)],
-                    dst_ref=values_in.at[pl.ds(0, liq_n), pl.ds(0, part)],
-                    send_sem=plane_send.at[0], recv_sem=plane_recv.at[slot_of(step, flip)],
-                    device_id=at(step, flip), device_id_type=MESH_ID,
-                ).wait_recv()
-
-    with scope("second"):
-        is_last = ill_me == ill_n - 1
-        for d in range(durables):
-            expected = []
-            for a in range(ill_rows + 1):
-                wide = jnp.concatenate([values_in[d * planes + a * liq_n + h] for h in range(liq_n)], axis=1)
-                expected.append(times(left_two, wide))
-            expected[ill_rows] = jnp.where(is_last, expected[ill_rows - 1], expected[ill_rows])
-            for a in range(ill_rows):
-                own = drift_ref[a]
-                found = lax.rsqrt(own * expected[a] + (1.0 - own) * expected[a + 1])
-                for h in range(liq_n):
-                    pencil_two[(d * ill_rows + a) * liq_n + h] = found[:, h * liq_rows : (h + 1) * liq_rows]
-        for k, (d, a) in enumerate(kinds):
+            depart_all(liq_n * ill_n).wait_send()
+
+    with scope("found"):
+        for flip in range(1, ill_n):
+            found_copy(flip).wait_send()
+            found_copy(flip).wait_recv()
             for q in range(liq_n):
-                base = (d * liq_n + q) * per_dest
-                blocks = [pencil_two[k * liq_n + h, pl.ds(q * part, part), :] for h in range(liq_n)]
-                consumption_ref[rows_at(d, a, q), :] = interpolate(
-                    blocks, near_out[base + ill_rows + a], near_out[base + 2 * ill_rows + a]
-                )
+                for a in range(ill_rows):
+                    consumption_ref[rows_at(peer_of(ill_me, flip, ill_n), a, q), :] = found_in[flip - 1, q * ill_rows + a]
 
     with scope("mass"):
-        for step, flip in peers:
-            mass_copy(step, flip).wait_recv()
+        mass_all().wait_recv()
 
         @pl.when(dur_me < dur_n - 1)
         def _():
-            for step in range(liq_n):
-                depart_copy(step, 0).wait_recv()
+            depart_all(liq_n).wait_recv()
 
     with scope("next"):
         settled = []
@@ -851,31 +868,6 @@
         for k, (d, a) in enumerate(kinds):
             for q in range(liq_n):
                 next_ref[rows_at(d, a, q), :] = found[q * part : (q + 1) * part, k * liq_rows : (k + 1) * liq_rows]
-
-    for flip in range(1, ill_n):
-        side_copy(flip).wait_send()
-    for step, flip in peers:
-        near_copy(step, flip).wait_send()
-        late_copy(step, flip).wait_send()
-        mass_copy(step, flip).wait_send()
-
-    for i in range(ill_n):
-        for step in range(1, liq_n):
-            main_copy(i, step).wait_send()
-            if i < ill_n - 1:
-                plane_copy(i, step).wait_send()
-
-        @pl.when(ill_me != i)
-        def _():
-            main_copy(i, 0).wait_send()
-            if i < ill_n - 1:
-                plane_copy(i, 0).wait_send()
-
-    @pl.when(departs)
-    def _():
-        for step in range(liq_n):
-            for i in range(ill_n):
-                depart_copy(step, i).wait_send()
 
 
 def store(consumption_ref, next_ref, consumption_hbm, next_hbm, sem):
@@ -952,8 +944,7 @@
     ill_all = ill_n * ill_rows
     tiles = lambda n: pltpu.VMEM((n, part, liq_rows), f32)
     slabs = lambda n: pltpu.VMEM((n, incomes, liq_rows), f32)
-    bundle = durables * liq_n * 3 * ill_rows
-    peers = liq_n * ill_n
+    bundles = pltpu.VMEM((durables * liq_n, 3 * ill_rows, part, liq_rows), f32)
     return [
         pltpu.VMEM(block, f32),
         pltpu.VMEM((incomes, incomes), f32),
@@ -968,25 +959,25 @@
         pltpu.SMEM((ill_rows,), f32),
         pltpu.SMEM((durables,), f32),
         dma((12,)),
-        tiles(bundle),
-        tiles(bundle),
-        tiles(bundle),
-        tiles(bundle),
+        bundles,
+        bundles,
+        bundles,
+        bundles,
         pltpu.VMEM((durables, ill_rows + 1, TILE, liq_rows), f32),
         pltpu.VMEM((ill_n, ill_rows + 1, TILE, liq_rows), f32),
+        pltpu.VMEM((ill_n, liq_n, 2 * ill_rows, part, liq_rows), f32),
         tiles(2 * ill_all * liq_n),
         tiles(ill_all * liq_n),
-        slabs(durables * (ill_rows + 1) * liq_n),
-        slabs(durables * ill_rows * liq_n),
+        slabs(ill_all * liq_n),
+        slabs(ill_all * liq_n),
+        pltpu.VMEM((ill_n - 1, liq_n * ill_rows, part, liq_rows), f32),
+        pltpu.VMEM((ill_n - 1, liq_n * ill_rows, part, liq_rows), f32),
         pltpu.VMEM((2 * liq_n * ill_all * part, liq_rows), f32),
         tiles(liq_n * ill_all),
         tiles(liq_n * ill_all),
         slabs((durables + 1) * ill_rows),
     ] + [
-        dma((n,))
-        for n in (
-            peers, peers, peers, peers, ill_n, ill_n, peers, peers, peers, peers, peers, peers, peers, liq_n,
-        )
+        dma((n,)) for n in (1, 1, 1, 1, ill_n - 1, ill_n - 1, ill_n - 1, ill_n - 1, 1, 1, ill_n - 1, ill_n - 1, 1, 1, 1, 1)
     ] + [pltpu.SemaphoreType.REGULAR]
 
 

time: 18.2 us -> 17.2 us (0.945)
  Pallas kernels: 17.3 us -> 16.3 us
    pallas_call x1, Pallas kernels: 16.6 us -> 15.7 us  [body(): pl.pallas_call(functools.partial(step_kernel, dims), out_shape=(held, hel...]
where the time goes in v2:
time: 17.2 us; the launch traced here: 17 us
  Pallas kernels  16.3 us (95%)
  between operations  0.64 us (4%)
    pallas_call x1, Pallas kernels, body(): pl.pallas_call(functools.partial(step_kernel, dims), out_shape=(held, hel...  15.7 us
    pallas_call x1, Pallas kernels, body(): pl.pallas_call(store, out_shape=(result, result), in_specs=[vmem, vmem],...  0.67 us

profile of v2, /device:TPU:0, one launch (start us, length us, event | category | flops | bytes accessed | tf_op | source)
XLA Modules:
  0.0 17.0 jit_solution(14986542931714878495)
XLA Ops:
  0.6 15.7 %transposed_window.1 = (f32[128,128]{1,0:T(8,128)S(1)}, f32[128,128]{1,0:T(8,128)S(1)}) custom-call(f32[128,128]{1,0:T(8,128)} %bitcast.13, f32[32,32]{1,0:T(8,128)} %transition_hbm.1, f32[1,32]{1,0:T(1,128)} %bitcast.21, f32[2]{0:T(128)} %drift_hbm.1, f32[2]{0:T(128)} %keep_hbm.1, s32[128,128]{1,0:T(8,128)} %bitcast.14, f32[128,128]{1,0:T(8,128)} %bitcast.15, ...), custom_call_target="tpu_custom_call" | custom-call | tf_op jit(solution)/shard_map/transposed_window/pallas_call | solution.py:1018
  16.3 0.7 %store.1 = (f32[128,128]{1,0:T(8,128)}, f32[128,128]{1,0:T(8,128)}) custom-call(f32[128,128]{1,0:T(8,128)S(1)} %get-tuple-element.6.consumption_ref, f32[128,128]{1,0:T(8,128)S(1)} %get-tuple-element.7.next_ref), custom_call_target="tpu_custom_call" | custom-call | tf_op jit(solution)/shard_map/store/pallas_call | solution.py:1040

commit v3 on v2

--- a/solution.py
+++ b/solution.py
@@ -432,8 +432,8 @@
     value_ref, transition_ref, shock_ref, index_ref, weight_ref, steady_ref, lottery_ref, target_ref,
     population_ref, ill_target_ref, drift_ref, keep_ref, load_sem,
     near_out, near_in, late_out, late_in, side_out, side_in, pair_in,
-    pencil_one, value_two, values_in, pencil_two, found_out, found_in, placed, mass_out, depart_out, mass_in,
-    near_send, near_recv, late_send, late_recv, side_send, side_recv, pair_send, pair_recv,
+    pencil_one, value_two, values_in, pencil_two, found_out, found_in, hots, placed, mass_out, depart_out, mass_in,
+    near_send, near_recv, late_send, late_recv, goal_send, goal_recv, side_send, side_recv, pair_send, pair_recv,
     value_send, value_recv, found_send, found_recv, mass_send, mass_recv, depart_send, depart_recv, ready_sem,
 ):
     incomes, durables, ill_rows, liq_rows, liq_n, ill_n, dur_n = dims
@@ -538,31 +538,38 @@
     def _():
         pl.semaphore_signal(ready_sem, inc=1, device_id={"dur": dur_me + 1}, device_id_type=MESH_ID)
 
-    def bundle_copy(out_ref, in_ref, send, recv, step, flip):
-        there = at(step, flip)
-        return pltpu.make_async_remote_copy(
-            src_ref=out_ref.at[there["ill"] * liq_n + there["liq"]], dst_ref=in_ref.at[liq_me * ill_n + ill_me],
+    def bundle_copy(out_ref, in_ref, send, recv, first, count, step, flip):
+        there, kept = at(step, flip), pl.ds(first, count)
+        return pltpu.make_async_remote_copy(
+            src_ref=out_ref.at[there["ill"] * liq_n + there["liq"], kept],
+            dst_ref=in_ref.at[liq_me * ill_n + ill_me, kept],
             send_sem=send.at[0], recv_sem=recv.at[0], device_id=there, device_id_type=MESH_ID,
         )
 
-    def bundle_all(out_ref, in_ref, send, recv):
-        span = pl.ds(0, len(peers))
-        return pltpu.make_async_remote_copy(
-            src_ref=out_ref.at[span], dst_ref=in_ref.at[span], send_sem=send.at[0], recv_sem=recv.at[0],
+    def bundle_all(out_ref, in_ref, send, recv, first, count):
+        span, kept = pl.ds(0, len(peers)), pl.ds(first, count)
+        return pltpu.make_async_remote_copy(
+            src_ref=out_ref.at[span, kept], dst_ref=in_ref.at[span, kept], send_sem=send.at[0], recv_sem=recv.at[0],
             device_id=at(0, 1), device_id_type=MESH_ID,
         )
 
     def near_all():
-        return bundle_all(near_out, near_in, near_send, near_recv)
+        return bundle_all(near_out, near_in, near_send, near_recv, 0, per_dest)
 
     def late_all():
-        return bundle_all(late_out, late_in, late_send, late_recv)
+        return bundle_all(late_out, late_in, late_send, late_recv, 0, 2 * ill_rows)
+
+    def goal_all():
+        return bundle_all(late_out, late_in, goal_send, goal_recv, 2 * ill_rows, ill_rows)
 
     def near_copy(step, flip):
-        return bundle_copy(near_out, near_in, near_send, near_recv, step, flip)
+        return bundle_copy(near_out, near_in, near_send, near_recv, 0, per_dest, step, flip)
 
     def late_copy(step, flip):
-        return bundle_copy(late_out, late_in, late_send, late_recv, step, flip)
+        return bundle_copy(late_out, late_in, late_send, late_recv, 0, 2 * ill_rows, step, flip)
+
+    def goal_copy(step, flip):
+        return bundle_copy(late_out, late_in, goal_send, goal_recv, 2 * ill_rows, ill_rows, step, flip)
 
     def side_copy(flip):
         there = at(0, flip)
@@ -592,6 +599,8 @@
             late_out[d * liq_n + q, a] = lottery_ref[span, :] - SLOPE_GAIN * steady_ref[span, :]
             late_out[d * liq_n + q, ill_rows + a] = population_ref[span, :]
             late_out[d * liq_n + q, 2 * ill_rows + a] = target_ref[span, :].astype(f32)
+    for step, flip in peers:
+        goal_copy(step, flip).start()
     for step, flip in peers:
         late_copy(step, flip).start()
     for flip in range(1, ill_n):
@@ -634,20 +643,22 @@
 
     own_z = pl.ds(pl.multiple_of(liq_me * part, TILE), part)
 
-    chunk = ill_rows * liq_n
-
-    def value_copy(i, step):
-        span = pl.ds(i * chunk, chunk)
+    ill_pair = peer_of(ill_me, 1, ill_n)
+    pieces = [(ill_pair * ill_rows, ill_rows)] + [(ill_me * ill_rows + a, 1) for a in range(ill_rows)]
+
+    def value_copy(k, step):
+        start, count = pieces[k]
+        span = pl.ds(start * liq_n, count * liq_n)
         return pltpu.make_async_remote_copy(
             src_ref=value_two.at[span], dst_ref=values_in.at[span, own_z], send_sem=value_send.at[0],
-            recv_sem=value_recv.at[0], device_id={"liq": peer_of(liq_me, step, liq_n)}, device_id_type=MESH_ID,
-        )
-
-    def value_all():
-        span = pl.ds(0, (liq_n - 1) * ill_all)
+            recv_sem=value_recv.at[k], device_id={"liq": peer_of(liq_me, step, liq_n)}, device_id_type=MESH_ID,
+        )
+
+    def value_all(k, count):
+        span = pl.ds(0, (liq_n - 1) * count)
         return pltpu.make_async_remote_copy(
             src_ref=values_in.at[span], dst_ref=values_in.at[span], send_sem=value_send.at[0],
-            recv_sem=value_recv.at[0], device_id=at(1, 0), device_id_type=MESH_ID,
+            recv_sem=value_recv.at[k], device_id=at(1, 0), device_id_type=MESH_ID,
         )
 
     with scope("near"):
@@ -662,81 +673,91 @@
             for h in range(liq_n):
                 drifted = own * received(near_in, 0, h, ag) + (1.0 - own) * received(near_in, 0, h, min(ag + 1, ill_all - 1))
                 pencil_one[ag * liq_n + h] = lax.rsqrt(drifted)
+        for k, (start, count) in enumerate(pieces):
+            for turn in range(count):
+                i, a = (ill_pair, turn) if k == 0 else (ill_me, k - 1)
+                ag = i * ill_rows + a
+                blocks = [pencil_one[ag * liq_n + h] for h in range(liq_n)]
+                for h in range(liq_n):
+                    source = h * ill_n + i
+                    chosen = interpolate(blocks, near_in[source, ill_rows + a], near_in[source, 2 * ill_rows + a])
+                    found = GROSS_RATE / (chosen * chosen)
+                    value_two[ag * liq_n + h] = found
+                    values_in[ag * liq_n + h, own_z, :] = found
+                    pencil_one[ill_all * liq_n + ag * liq_n + h] = chosen
+            for step in far_first:
+                value_copy(k, step).start()
+
+    half = liq_rows // 2
+    cuts = 2 * liq_n
+    sub = iota((cuts, liq_rows), 0).astype(f32)
+    lane_at = iota((TILE, liq_rows), 1)
+    lane_row = iota((half, liq_rows), 0).astype(f32).astype(jnp.bfloat16)
+    one = jnp.ones((half, liq_rows), jnp.bfloat16)
+    nil = jnp.zeros((half, liq_rows), jnp.bfloat16)
+
+    with scope("goal"):
+        goal_all().wait_recv()
+    with scope("hots"):
+        cut_at = {}
         for ag in range(ill_all):
-            blocks = [pencil_one[ag * liq_n + h] for h in range(liq_n)]
+            places = []
             for h in range(liq_n):
-                chosen = interpolate(blocks, received(near_in, 1, h, ag), received(near_in, 2, h, ag))
-                found = GROSS_RATE / (chosen * chosen)
-                value_two[ag * liq_n + h] = found
-                values_in[ag * liq_n + h, own_z, :] = found
-                pencil_one[ill_all * liq_n + ag * liq_n + h] = chosen
-            if ag % ill_rows == ill_rows - 1:
-                for step in far_first:
-                    value_copy(ag // ill_rows, step).start()
-
-    lanes = 2 * liq_n
-    sub = iota((lanes, liq_rows), 0)
-    lane_at = iota((TILE, liq_rows), 1)
-    sub_block = jnp.where(sub < liq_n, sub, sub - liq_n).astype(f32)
-    lane_row = iota((liq_rows, liq_rows), 0).astype(f32).astype(jnp.bfloat16)
-    one = jnp.ones((liq_rows, liq_rows), jnp.bfloat16)
-    nil = jnp.zeros((liq_rows, liq_rows), jnp.bfloat16)
-
-    def scattered(steps):
+                target = received(late_in, 2, h, ag)
+                cut = jnp.zeros(target.shape, f32)
+                for other in range(1, cuts):
+                    cut = cut + jnp.where(target >= other * half, 1.0, 0.0)
+                cut_at[ag, h] = cut
+                places.append(target - half * cut)
+            for s in range(part):
+                for h in range(liq_n):
+                    place = jnp.broadcast_to(places[h][s : s + 1, :], (2 * TILE, liq_rows)).astype(jnp.bfloat16)
+                    place = jnp.concatenate([place] * (half // (2 * TILE)), axis=0)
+                    hots[s * ill_all + ag, :, h * liq_rows : (h + 1) * liq_rows] = jnp.where(lane_row == place, one, nil)
+    with scope("late"):
+        late_all().wait_recv()
+    with scope("scatter"):
         held = {}
         for ag in range(ill_all):
-            for step in steps:
-                h = step
+            for h in range(liq_n):
                 chosen = pencil_one[ill_all * liq_n + ag * liq_n + h]
                 share = jnp.clip(received(late_in, 0, h, ag) + SLOPE_GAIN * chosen, 0.0, 1.0)
                 mass = received(late_in, 1, h, ag)
-                target = received(late_in, 2, h, ag)
-                block = jnp.zeros(target.shape, f32)
-                for other in range(1, liq_n):
-                    block = block + jnp.where(target >= other * liq_rows, 1.0, 0.0)
-                held[ag, step] = (mass * share, mass * (1.0 - share), block, target - liq_rows * block)
+                held[ag, h] = (mass * share, mass * (1.0 - share), cut_at[ag, h])
         for s in range(part):
+            totals, to_row = [], []
             for ag in range(ill_all):
-                lefts, hots = [], []
-                for step in steps:
-                    low_t, high_t, hi_t, lo_t = (x[s : s + 1, :] for x in held[ag, step])
-                    both = jnp.where(sub < liq_n, low_t, high_t)
-                    both = jnp.where(hi_t == sub_block, both, 0.0)
-                    rounded = both.astype(jnp.bfloat16).astype(f32)
-                    lefts.append(jnp.concatenate([both, both - rounded], axis=0).astype(jnp.bfloat16))
-                    place = jnp.broadcast_to(lo_t, (2 * TILE, liq_rows)).astype(jnp.bfloat16)
-                    place = jnp.concatenate([place] * (liq_rows // (2 * TILE)), axis=0)
-                    hots.append(jnp.where(lane_row == place, one, nil))
+                lefts = []
+                for h in range(liq_n):
+                    low_t, high_t, cut_t = (x[s : s + 1, :] for x in held[ag, h])
+                    here = cut_t == sub
+                    both = jnp.concatenate([jnp.where(here, low_t, 0.0), jnp.where(here, high_t, 0.0)], axis=0)
+                    first = both.astype(jnp.bfloat16)
+                    lefts.append(jnp.concatenate([first, (both - first.astype(f32)).astype(jnp.bfloat16)], axis=0))
                 found = lax.dot_general(
-                    jnp.concatenate(lefts, axis=1), jnp.concatenate(hots, axis=1), NT, preferred_element_type=f32
+                    jnp.concatenate(lefts, axis=1), hots[s * ill_all + ag], NT, preferred_element_type=f32
                 )
-                yield s, ag, found[:lanes] + found[lanes:]
-
-    with scope("late"):
-        late_all().wait_recv()
-    with scope("scatter"):
-        totals = []
-        for s, ag, total in scattered(range(liq_n)):
-            totals.append(total)
-            if ag == ill_all - 1:
-                to_row = [
-                    jnp.broadcast_to(side_in[k // ill_rows, k % ill_rows, s : s + 1, :], (lanes, liq_rows))
-                    for k in range(ill_all)
-                ]
-                for dest in range(ill_all):
-                    out = None
-                    for k in range(ill_all):
-                        here = jnp.where(to_row[k] == dest, totals[k], 0.0)
-                        out = here if out is None else out + here
-                    placed[pl.ds(dest * part + s, lanes, stride=ill_all * part), :] = out
-                totals = []
+                totals.append(found[: 2 * cuts] + found[2 * cuts :])
+                to_row.append(jnp.broadcast_to(side_in[ag // ill_rows, ag % ill_rows, s : s + 1, :half], (2 * cuts, half)))
+            for dest in range(ill_all):
+                out = None
+                for ag in range(ill_all):
+                    here = jnp.where(to_row[ag] == dest, totals[ag], 0.0)
+                    out = here if out is None else out + here
+                placed[pl.ds(dest * 2 * cuts * part + s, 2 * cuts, stride=part), :half] = out
 
     with scope("massout"):
+        def joined(dest, side, h):
+            start = ((dest * 2 + side) * cuts + 2 * h) * part
+            return jnp.concatenate(
+                [placed[pl.ds(start, part), :half], placed[pl.ds(start + part, part), :half]], axis=1
+            )
+
         for dest in range(ill_all):
             carried = None
             for h in range(liq_n):
-                low = placed[pl.ds((h * ill_all + dest) * part, part), :]
-                moved = pltpu.roll(placed[pl.ds(((liq_n + h) * ill_all + dest) * part, part), :], 1, 1)
+                low = joined(dest, 0, h)
+                moved = pltpu.roll(joined(dest, 1, h), 1, 1)
                 total = low + jnp.where(lane_at > 0, moved, 0.0 if carried is None else carried)
                 carried = moved
                 mass_out[h * ill_all + dest] = total
@@ -800,38 +821,60 @@
         pair_copy(flip).wait_recv()
     near_all().wait_send()
     late_all().wait_send()
-    with scope("values"):
-        value_all().wait_recv()
-
-    with scope("second"):
-        expected = []
-        for ag in range(ill_all):
-            wide = jnp.concatenate([values_in[ag * liq_n + h] for h in range(liq_n)], axis=1)
-            expected.append(times(left_two, wide))
-        for ag in range(ill_all):
-            i, a = divmod(ag, ill_rows)
+    goal_all().wait_send()
+    is_last = ill_me == ill_n - 1
+
+    def expect(ag):
+        wide = jnp.concatenate([values_in[ag * liq_n + h] for h in range(liq_n)], axis=1)
+        return times(left_two, wide)
+
+    def consume(i, expected, store_tile):
+        for a in range(ill_rows):
             own = jnp.broadcast_to(side_in[i, ill_rows, a : a + 1, :], (incomes, liq_rows))
             own = jnp.concatenate([own] * liq_n, axis=1)
-            found = lax.rsqrt(own * expected[ag] + (1.0 - own) * expected[min(ag + 1, ill_all - 1)])
+            found = lax.rsqrt(own * expected[a] + (1.0 - own) * expected[a + 1])
             for h in range(liq_n):
-                pencil_two[ag * liq_n + h] = found[:, h * liq_rows : (h + 1) * liq_rows]
-        for flip in range(ill_n - 1, -1, -1):
-            i = peer_of(ill_me, flip, ill_n)
-            for a in range(ill_rows):
-                for q in range(liq_n):
-                    blocks = [
-                        pencil_two[(i * ill_rows + a) * liq_n + h, pl.ds(q * part, part), :] for h in range(liq_n)
-                    ]
-                    found = interpolate(blocks, pair_in[i, q, a], pair_in[i, q, ill_rows + a])
-                    if flip:
-                        found_out[flip - 1, q * ill_rows + a] = found
-                    else:
-                        consumption_ref[rows_at(ill_me, a, q), :] = found
-            if flip:
-                found_copy(flip).start()
+                pencil_two[a * liq_n + h] = found[:, h * liq_rows : (h + 1) * liq_rows]
+        for a in range(ill_rows):
+            for q in range(liq_n):
+                blocks = [pencil_two[a * liq_n + h, pl.ds(q * part, part), :] for h in range(liq_n)]
+                store_tile(a, q, interpolate(blocks, pair_in[i, q, a], pair_in[i, q, ill_rows + a]))
+
+    def store_found(a, q, found):
+        found_out[0, q * ill_rows + a] = found
+
+    def store_own(a, q, found):
+        consumption_ref[rows_at(ill_me, a, q), :] = found
+
+    with scope("values"):
+        value_all(0, ill_rows).wait_recv()
+
+        @pl.when(is_last)
+        def _():
+            value_all(1, 1).wait_recv()
+
+    with scope("second_a"):
+        above = jnp.minimum(ill_pair * ill_rows + ill_rows, ill_all - 1)
+        expected = [expect(ill_pair * ill_rows + a) for a in range(ill_rows)]
+        lowest = expected[0]
+        consume(ill_pair, expected + [expect(above)], store_found)
+        found_copy(1).start()
+
+    with scope("values_b"):
+        @pl.when(jnp.logical_not(is_last))
+        def _():
+            value_all(1, 1).wait_recv()
+
+        for a in range(1, ill_rows):
+            value_all(1 + a, 1).wait_recv()
+
+    with scope("second_b"):
+        expected = [expect(ill_me * ill_rows + a) for a in range(ill_rows)]
+        expected.append(jnp.where(is_last, expected[-1], lowest))
+        consume(ill_me, expected, store_own)
 
     with scope("sends"):
-        value_all().wait_send()
+        value_all(0, ill_all).wait_send()
         mass_all().wait_send()
 
         @pl.when(departs)
@@ -969,15 +1012,16 @@
         tiles(2 * ill_all * liq_n),
         tiles(ill_all * liq_n),
         slabs(ill_all * liq_n),
-        slabs(ill_all * liq_n),
+        slabs(ill_rows * liq_n),
         pltpu.VMEM((ill_n - 1, liq_n * ill_rows, part, liq_rows), f32),
         pltpu.VMEM((ill_n - 1, liq_n * ill_rows, part, liq_rows), f32),
-        pltpu.VMEM((2 * liq_n * ill_all * part, liq_rows), f32),
+        pltpu.VMEM((part * ill_all, liq_rows // 2, liq_n * liq_rows), jnp.bfloat16),
+        pltpu.VMEM((4 * liq_n * ill_all * part, liq_rows), f32),
         tiles(liq_n * ill_all),
         tiles(liq_n * ill_all),
         slabs((durables + 1) * ill_rows),
     ] + [
-        dma((n,)) for n in (1, 1, 1, 1, ill_n - 1, ill_n - 1, ill_n - 1, ill_n - 1, 1, 1, ill_n - 1, ill_n - 1, 1, 1, 1, 1)
+        dma((n,)) for n in (1, 1, 1, 1, 1, 1, 1, 1, 1, 1, 1, ill_rows + 1, 1, 1, 1, 1, 1, 1)
     ] + [pltpu.SemaphoreType.REGULAR]
 
 

time: 17.2 us -> 17.1 us (level)
  no operation moved by 1% of the time
where the time goes in v3:
time: 17.1 us; the launch traced here: 16.8 us
  Pallas kernels  16.2 us (95%)
  between operations  0.64 us (4%)
    pallas_call x1, Pallas kernels, body(): pl.pallas_call(functools.partial(step_kernel, dims), out_shape=(held, hel...  15.5 us
    pallas_call x1, Pallas kernels, body(): pl.pallas_call(store, out_shape=(result, result), in_specs=[vmem, vmem],...  0.67 us

profile of v3, /device:TPU:0, one launch (start us, length us, event | category | flops | bytes accessed | tf_op | source)
XLA Modules:
  0.0 16.8 jit_solution(986236047850888592)
XLA Ops:
  0.6 15.5 %transposed_window.1 = (f32[128,128]{1,0:T(8,128)S(1)}, f32[128,128]{1,0:T(8,128)S(1)}) custom-call(f32[128,128]{1,0:T(8,128)} %bitcast.13, f32[32,32]{1,0:T(8,128)} %transition_hbm.1, f32[1,32]{1,0:T(1,128)} %bitcast.21, f32[2]{0:T(128)} %drift_hbm.1, f32[2]{0:T(128)} %keep_hbm.1, s32[128,128]{1,0:T(8,128)} %bitcast.14, f32[128,128]{1,0:T(8,128)} %bitcast.15, ...), custom_call_target="tpu_custom_call" | custom-call | tf_op jit(solution)/shard_map/transposed_window/pallas_call | solution.py:1062
  16.2 0.7 %store.1 = (f32[128,128]{1,0:T(8,128)}, f32[128,128]{1,0:T(8,128)}) custom-call(f32[128,128]{1,0:T(8,128)S(1)} %get-tuple-element.6.consumption_ref, f32[128,128]{1,0:T(8,128)S(1)} %get-tuple-element.7.next_ref), custom_call_target="tpu_custom_call" | custom-call | tf_op jit(solution)/shard_map/store/pallas_call | solution.py:1084

commit v4 on v3

--- a/solution.py
+++ b/solution.py
@@ -538,12 +538,11 @@
     def _():
         pl.semaphore_signal(ready_sem, inc=1, device_id={"dur": dur_me + 1}, device_id_type=MESH_ID)
 
-    def bundle_copy(out_ref, in_ref, send, recv, first, count, step, flip):
-        there, kept = at(step, flip), pl.ds(first, count)
-        return pltpu.make_async_remote_copy(
-            src_ref=out_ref.at[there["ill"] * liq_n + there["liq"], kept],
-            dst_ref=in_ref.at[liq_me * ill_n + ill_me, kept],
-            send_sem=send.at[0], recv_sem=recv.at[0], device_id=there, device_id_type=MESH_ID,
+    def bundle_copy(out_ref, in_ref, send, recv, first, count, step, i):
+        liq_there, kept = peer_of(liq_me, step, liq_n), pl.ds(first, count)
+        return pltpu.make_async_remote_copy(
+            src_ref=out_ref.at[i * liq_n + liq_there, kept], dst_ref=in_ref.at[liq_me * ill_n + ill_me, kept],
+            send_sem=send.at[0], recv_sem=recv.at[0], device_id={"liq": liq_there, "ill": i}, device_id_type=MESH_ID,
         )
 
     def bundle_all(out_ref, in_ref, send, recv, first, count):
@@ -562,14 +561,14 @@
     def goal_all():
         return bundle_all(late_out, late_in, goal_send, goal_recv, 2 * ill_rows, ill_rows)
 
-    def near_copy(step, flip):
-        return bundle_copy(near_out, near_in, near_send, near_recv, 0, per_dest, step, flip)
-
-    def late_copy(step, flip):
-        return bundle_copy(late_out, late_in, late_send, late_recv, 0, 2 * ill_rows, step, flip)
-
-    def goal_copy(step, flip):
-        return bundle_copy(late_out, late_in, goal_send, goal_recv, 2 * ill_rows, ill_rows, step, flip)
+    def near_copy(step, i):
+        return bundle_copy(near_out, near_in, near_send, near_recv, 0, per_dest, step, i)
+
+    def late_copy(step, i):
+        return bundle_copy(late_out, late_in, late_send, late_recv, 0, 2 * ill_rows, step, i)
+
+    def goal_copy(step, i):
+        return bundle_copy(late_out, late_in, goal_send, goal_recv, 2 * ill_rows, ill_rows, step, i)
 
     def side_copy(flip):
         there = at(0, flip)
@@ -586,8 +585,16 @@
             device_id=there, device_id_type=MESH_ID,
         )
 
-    for step, flip in peers:
-        near_copy(step, flip).start()
+    def start_to(i, make):
+        for step in far_first:
+            make(step, i).start()
+
+        @pl.when(ill_me != i)
+        def _():
+            make(0, i).start()
+
+    for i in range(ill_n):
+        start_to(i, near_copy)
     for flip in range(1, ill_n):
         side_copy(flip).start()
 
@@ -599,10 +606,9 @@
             late_out[d * liq_n + q, a] = lottery_ref[span, :] - SLOPE_GAIN * steady_ref[span, :]
             late_out[d * liq_n + q, ill_rows + a] = population_ref[span, :]
             late_out[d * liq_n + q, 2 * ill_rows + a] = target_ref[span, :].astype(f32)
-    for step, flip in peers:
-        goal_copy(step, flip).start()
-    for step, flip in peers:
-        late_copy(step, flip).start()
+    for i in range(ill_n):
+        start_to(i, goal_copy)
+        start_to(i, late_copy)
     for flip in range(1, ill_n):
         pair_copy(flip).start()
 

time: 17.1 us -> 16.8 us (0.982)
  Pallas kernels: 16.2 us -> 15.9 us
    pallas_call x1, Pallas kernels: 15.5 us -> 15.2 us  [body(): pl.pallas_call(functools.partial(step_kernel, dims), out_shape=(held, hel...]
where the time goes in v4:
time: 16.8 us; the launch traced here: 16.5 us
  Pallas kernels  15.9 us (95%)
  between operations  0.64 us (4%)
    pallas_call x1, Pallas kernels, body(): pl.pallas_call(functools.partial(step_kernel, dims), out_shape=(held, hel...  15.2 us
    pallas_call x1, Pallas kernels, body(): pl.pallas_call(store, out_shape=(result, result), in_specs=[vmem, vmem],...  0.67 us

profile of v4, /device:TPU:0, one launch (start us, length us, event | category | flops | bytes accessed | tf_op | source)
XLA Modules:
  0.0 16.5 jit_solution(9648059460447998663)
XLA Ops:
  0.6 15.2 %transposed_window.1 = (f32[128,128]{1,0:T(8,128)S(1)}, f32[128,128]{1,0:T(8,128)S(1)}) custom-call(f32[128,128]{1,0:T(8,128)} %bitcast.13, f32[32,32]{1,0:T(8,128)} %transition_hbm.1, f32[1,32]{1,0:T(1,128)} %bitcast.21, f32[2]{0:T(128)} %drift_hbm.1, f32[2]{0:T(128)} %keep_hbm.1, s32[128,128]{1,0:T(8,128)} %bitcast.14, f32[128,128]{1,0:T(8,128)} %bitcast.15, ...), custom_call_target="tpu_custom_call" | custom-call | tf_op jit(solution)/shard_map/transposed_window/pallas_call | solution.py:1068
  15.9 0.7 %store.1 = (f32[128,128]{1,0:T(8,128)}, f32[128,128]{1,0:T(8,128)}) custom-call(f32[128,128]{1,0:T(8,128)S(1)} %get-tuple-element.6.consumption_ref, f32[128,128]{1,0:T(8,128)S(1)} %get-tuple-element.7.next_ref), custom_call_target="tpu_custom_call" | custom-call | tf_op jit(solution)/shard_map/store/pallas_call | solution.py:1090

commit v5 on v4

--- a/solution.py
+++ b/solution.py
@@ -585,16 +585,17 @@
             device_id=there, device_id_type=MESH_ID,
         )
 
-    def start_to(i, make):
-        for step in far_first:
+    def start_far(i, make):
+        make(liq_n - 1, i).start()
+
+    def start_close(i, make):
+        for step in range(liq_n - 2, 0, -1):
             make(step, i).start()
 
         @pl.when(ill_me != i)
         def _():
             make(0, i).start()
 
-    for i in range(ill_n):
-        start_to(i, near_copy)
     for flip in range(1, ill_n):
         side_copy(flip).start()
 
@@ -606,9 +607,21 @@
             late_out[d * liq_n + q, a] = lottery_ref[span, :] - SLOPE_GAIN * steady_ref[span, :]
             late_out[d * liq_n + q, ill_rows + a] = population_ref[span, :]
             late_out[d * liq_n + q, 2 * ill_rows + a] = target_ref[span, :].astype(f32)
-    for i in range(ill_n):
-        start_to(i, goal_copy)
-        start_to(i, late_copy)
+    start_far(0, near_copy)
+    start_far(0, goal_copy)
+    start_close(0, near_copy)
+    start_close(0, goal_copy)
+    for i in range(1, ill_n):
+        start_far(i, near_copy)
+    start_far(0, late_copy)
+    for i in range(1, ill_n):
+        start_close(i, near_copy)
+    start_close(0, late_copy)
+    for i in range(1, ill_n):
+        start_far(i, goal_copy)
+        start_far(i, late_copy)
+        start_close(i, goal_copy)
+        start_close(i, late_copy)
     for flip in range(1, ill_n):
         pair_copy(flip).start()
 
@@ -649,11 +662,14 @@
 
     own_z = pl.ds(pl.multiple_of(liq_me * part, TILE), part)
 
-    ill_pair = peer_of(ill_me, 1, ill_n)
-    pieces = [(ill_pair * ill_rows, ill_rows)] + [(ill_me * ill_rows + a, 1) for a in range(ill_rows)]
-
-    def value_copy(k, step):
-        start, count = pieces[k]
+    def pieces_of(me):
+        pair = (me + 1) % ill_n
+        first = (pair * ill_rows, min(ill_rows + 1, ill_all - pair * ill_rows))
+        rest = [ag for ag in range(ill_all) if not first[0] <= ag < sum(first)]
+        return [first, (rest[0], len(rest))]
+
+    def value_copy(me, k, step):
+        start, count = pieces_of(me)[k]
         span = pl.ds(start * liq_n, count * liq_n)
         return pltpu.make_async_remote_copy(
             src_ref=value_two.at[span], dst_ref=values_in.at[span, own_z], send_sem=value_send.at[0],
@@ -666,6 +682,13 @@
             src_ref=values_in.at[span], dst_ref=values_in.at[span], send_sem=value_send.at[0],
             recv_sem=value_recv.at[k], device_id=at(1, 0), device_id_type=MESH_ID,
         )
+
+    def on_each_core(part_of):
+        for me in range(ill_n):
+
+            @pl.when(ill_me == me)
+            def _():
+                part_of(me)
 
     with scope("near"):
         for flip in range(1, ill_n):
@@ -679,20 +702,36 @@
             for h in range(liq_n):
                 drifted = own * received(near_in, 0, h, ag) + (1.0 - own) * received(near_in, 0, h, min(ag + 1, ill_all - 1))
                 pencil_one[ag * liq_n + h] = lax.rsqrt(drifted)
-        for k, (start, count) in enumerate(pieces):
-            for turn in range(count):
-                i, a = (ill_pair, turn) if k == 0 else (ill_me, k - 1)
-                ag = i * ill_rows + a
-                blocks = [pencil_one[ag * liq_n + h] for h in range(liq_n)]
-                for h in range(liq_n):
-                    source = h * ill_n + i
-                    chosen = interpolate(blocks, near_in[source, ill_rows + a], near_in[source, 2 * ill_rows + a])
-                    found = GROSS_RATE / (chosen * chosen)
-                    value_two[ag * liq_n + h] = found
-                    values_in[ag * liq_n + h, own_z, :] = found
-                    pencil_one[ill_all * liq_n + ag * liq_n + h] = chosen
-            for step in far_first:
-                value_copy(k, step).start()
+
+        def policy(me):
+            pieces = pieces_of(me)
+
+            def loaded(k):
+                start, count = pieces[k]
+                return [
+                    (
+                        ag,
+                        [pencil_one[ag * liq_n + h] for h in range(liq_n)],
+                        [(received(near_in, 1, h, ag), received(near_in, 2, h, ag)) for h in range(liq_n)],
+                    )
+                    for ag in range(start, start + count)
+                ]
+
+            ahead = loaded(0)
+            for k in range(len(pieces)):
+                for ag, blocks, states in ahead:
+                    for h, (index, weight) in enumerate(states):
+                        chosen = interpolate(blocks, index, weight)
+                        found = GROSS_RATE / (chosen * chosen)
+                        value_two[ag * liq_n + h] = found
+                        values_in[ag * liq_n + h, own_z, :] = found
+                        pencil_one[ill_all * liq_n + ag * liq_n + h] = chosen
+                ahead = loaded(k + 1) if k + 1 < len(pieces) else []
+                for step in far_first:
+                    if k == 0 or step == liq_n - 1 or me > 0:
+                        value_copy(me, k, step).start()
+
+        on_each_core(policy)
 
     half = liq_rows // 2
     cuts = 2 * liq_n
@@ -809,6 +848,12 @@
             for i in range(ill_n):
                 depart_copy(step, i).start()
 
+    def send_rest(me):
+        for step in range(liq_n - 2, 0, -1):
+            value_copy(me, 1, step).start()
+
+    pl.when(ill_me == 0)(functools.partial(send_rest, 0))
+
     for step, flip in peers:
         mass_copy(step, flip).start()
     for a in range(ill_rows):
@@ -828,8 +873,6 @@
     near_all().wait_send()
     late_all().wait_send()
     goal_all().wait_send()
-    is_last = ill_me == ill_n - 1
-
     def expect(ag):
         wide = jnp.concatenate([values_in[ag * liq_n + h] for h in range(liq_n)], axis=1)
         return times(left_two, wide)
@@ -852,32 +895,25 @@
     def store_own(a, q, found):
         consumption_ref[rows_at(ill_me, a, q), :] = found
 
-    with scope("values"):
-        value_all(0, ill_rows).wait_recv()
-
-        @pl.when(is_last)
-        def _():
-            value_all(1, 1).wait_recv()
-
-    with scope("second_a"):
-        above = jnp.minimum(ill_pair * ill_rows + ill_rows, ill_all - 1)
-        expected = [expect(ill_pair * ill_rows + a) for a in range(ill_rows)]
-        lowest = expected[0]
-        consume(ill_pair, expected + [expect(above)], store_found)
-        found_copy(1).start()
-
-    with scope("values_b"):
-        @pl.when(jnp.logical_not(is_last))
-        def _():
-            value_all(1, 1).wait_recv()
-
-        for a in range(1, ill_rows):
-            value_all(1 + a, 1).wait_recv()
-
-    with scope("second_b"):
-        expected = [expect(ill_me * ill_rows + a) for a in range(ill_rows)]
-        expected.append(jnp.where(is_last, expected[-1], lowest))
-        consume(ill_me, expected, store_own)
+    def second(me):
+        pair, is_last = (me + 1) % ill_n, me == ill_n - 1
+        with scope("values"):
+            value_all(0, pieces_of(me)[0][1]).wait_recv()
+        with scope("second_a"):
+            expected = [expect(pair * ill_rows + a) for a in range(ill_rows)]
+            lowest = expected[0]
+            above = pair * ill_rows + ill_rows
+            expected.append(expected[-1] if above == ill_all else expect(above))
+            consume(pair, expected, store_found)
+            found_copy(1).start()
+        with scope("values_b"):
+            value_all(1, pieces_of(me)[1][1]).wait_recv()
+        with scope("second_b"):
+            expected = [expect(me * ill_rows + a) for a in range(ill_rows)]
+            expected.append(expected[-1] if is_last else lowest)
+            consume(me, expected, store_own)
+
+    on_each_core(second)
 
     with scope("sends"):
         value_all(0, ill_all).wait_send()
@@ -1027,7 +1063,7 @@
         tiles(liq_n * ill_all),
         slabs((durables + 1) * ill_rows),
     ] + [
-        dma((n,)) for n in (1, 1, 1, 1, 1, 1, 1, 1, 1, 1, 1, ill_rows + 1, 1, 1, 1, 1, 1, 1)
+        dma((n,)) for n in (1, 1, 1, 1, 1, 1, 1, 1, 1, 1, 1, 2, 1, 1, 1, 1, 1, 1)
     ] + [pltpu.SemaphoreType.REGULAR]
 
 

time: 16.8 us -> 16.6 us (0.988)
  Pallas kernels: 15.9 us -> 15.7 us
    pallas_call x1, Pallas kernels: 15.2 us -> 15 us  [body(): pl.pallas_call(functools.partial(step_kernel, dims), out_shape=(held, hel...]
where the time goes in v5:
time: 16.6 us; the launch traced here: 16.3 us
  Pallas kernels  15.7 us (95%)
  between operations  0.64 us (4%)
    pallas_call x1, Pallas kernels, body(): pl.pallas_call(functools.partial(step_kernel, dims), out_shape=(held, hel...  15 us
    pallas_call x1, Pallas kernels, body(): pl.pallas_call(store, out_shape=(result, result), in_specs=[vmem, vmem],...  0.67 us

profile of v5, /device:TPU:0, one launch (start us, length us, event | category | flops | bytes accessed | tf_op | source)
XLA Modules:
  0.0 16.3 jit_solution(4800087260351202625)
XLA Ops:
  0.6 15.0 %transposed_window.1 = (f32[128,128]{1,0:T(8,128)S(1)}, f32[128,128]{1,0:T(8,128)S(1)}) custom-call(f32[128,128]{1,0:T(8,128)} %bitcast.13, f32[32,32]{1,0:T(8,128)} %transition_hbm.1, f32[1,32]{1,0:T(1,128)} %bitcast.21, f32[2]{0:T(128)} %drift_hbm.1, f32[2]{0:T(128)} %keep_hbm.1, s32[128,128]{1,0:T(8,128)} %bitcast.14, f32[128,128]{1,0:T(8,128)} %bitcast.15, ...), custom_call_target="tpu_custom_call" | custom-call | tf_op jit(solution)/shard_map/transposed_window/pallas_call | solution.py:1104
  15.7 0.7 %store.1 = (f32[128,128]{1,0:T(8,128)}, f32[128,128]{1,0:T(8,128)}) custom-call(f32[128,128]{1,0:T(8,128)S(1)} %get-tuple-element.6.consumption_ref, f32[128,128]{1,0:T(8,128)S(1)} %get-tuple-element.7.next_ref), custom_call_target="tpu_custom_call" | custom-call | tf_op jit(solution)/shard_map/store/pallas_call | solution.py:1126

commit v6 on v5

--- a/solution.py
+++ b/solution.py
@@ -433,7 +433,7 @@
     population_ref, ill_target_ref, drift_ref, keep_ref, load_sem,
     near_out, near_in, late_out, late_in, side_out, side_in, pair_in,
     pencil_one, value_two, values_in, pencil_two, found_out, found_in, hots, placed, mass_out, depart_out, mass_in,
-    near_send, near_recv, late_send, late_recv, goal_send, goal_recv, side_send, side_recv, pair_send, pair_recv,
+    near_send, near_recv, late_send, late_recv, goal_recv, side_send, side_recv, pair_send, pair_recv,
     value_send, value_recv, found_send, found_recv, mass_send, mass_recv, depart_send, depart_recv, ready_sem,
 ):
     incomes, durables, ill_rows, liq_rows, liq_n, ill_n, dur_n = dims
@@ -464,15 +464,19 @@
 
     loads = [
         pltpu.make_async_copy(source, held, load_sem.at[slot])
-        for slot, (source, held) in enumerate((
-            (transition_hbm, transition_ref), (shock_hbm, shock_ref), (value_hbm, value_ref),
-            (index_hbm, index_ref), (weight_hbm, weight_ref), (drift_hbm, drift_ref), (ill_target_hbm, ill_target_ref),
-            (target_hbm, target_ref), (lottery_hbm, lottery_ref), (steady_hbm, steady_ref),
-            (population_hbm, population_ref), (keep_hbm, keep_ref),
-        ))
+        for slot, source, held in (
+            (0, transition_hbm, transition_ref), (1, shock_hbm, shock_ref), (2, value_hbm, value_ref),
+            (3, index_hbm, index_ref), (3, weight_hbm, weight_ref), (4, drift_hbm, drift_ref),
+            (5, ill_target_hbm, ill_target_ref), (6, target_hbm, target_ref), (6, lottery_hbm, lottery_ref),
+            (6, steady_hbm, steady_ref), (6, population_hbm, population_ref), (7, keep_hbm, keep_ref),
+        )
     ]
     for load in loads:
         load.start()
+
+    def load_all(slot, count):
+        span = pl.ds(0, count * group)
+        pltpu.make_async_copy(values_in.at[span], values_in.at[span], load_sem.at[slot]).wait()
 
     def rows_at(d, a, z_part):
         return pl.ds(z_part * part * group + d * ill_rows + a, part, stride=group)
@@ -499,8 +503,7 @@
     loads[2].wait()
     wide = jnp.concatenate([value_ref[whole_rows(d, a), :] for d, a in kinds], axis=1)
     wide = times(left_one, wide)
-    for load in loads[3:5]:
-        load.wait()
+    load_all(3, 2)
     for k, (d, a) in enumerate(kinds):
         for q in range(liq_n):
             near_out[d * liq_n + q, a] = wide[q * part : (q + 1) * part, k * liq_rows : (k + 1) * liq_rows]
@@ -559,7 +562,7 @@
         return bundle_all(late_out, late_in, late_send, late_recv, 0, 2 * ill_rows)
 
     def goal_all():
-        return bundle_all(late_out, late_in, goal_send, goal_recv, 2 * ill_rows, ill_rows)
+        return bundle_all(late_out, late_in, late_send, goal_recv, 2 * ill_rows, ill_rows)
 
     def near_copy(step, i):
         return bundle_copy(near_out, near_in, near_send, near_recv, 0, per_dest, step, i)
@@ -568,7 +571,7 @@
         return bundle_copy(late_out, late_in, late_send, late_recv, 0, 2 * ill_rows, step, i)
 
     def goal_copy(step, i):
-        return bundle_copy(late_out, late_in, goal_send, goal_recv, 2 * ill_rows, ill_rows, step, i)
+        return bundle_copy(late_out, late_in, late_send, goal_recv, 2 * ill_rows, ill_rows, step, i)
 
     def side_copy(flip):
         there = at(0, flip)
@@ -599,8 +602,8 @@
     for flip in range(1, ill_n):
         side_copy(flip).start()
 
-    for load in loads[7:]:
-        load.wait()
+    load_all(6, 4)
+    loads[11].wait()
     for d, a in kinds:
         for q in range(liq_n):
             span = rows_at(d, a, q)
@@ -871,8 +874,7 @@
         pair_copy(flip).wait_send()
         pair_copy(flip).wait_recv()
     near_all().wait_send()
-    late_all().wait_send()
-    goal_all().wait_send()
+    bundle_all(late_out, late_in, late_send, late_recv, 0, per_dest).wait_send()
     def expect(ag):
         wide = jnp.concatenate([values_in[ag * liq_n + h] for h in range(liq_n)], axis=1)
         return times(left_two, wide)
@@ -1043,7 +1045,7 @@
         pltpu.VMEM((durables * ill_rows, incomes), jnp.int32),
         pltpu.SMEM((ill_rows,), f32),
         pltpu.SMEM((durables,), f32),
-        dma((12,)),
+        dma((8,)),
         bundles,
         bundles,
         bundles,
@@ -1063,7 +1065,7 @@
         tiles(liq_n * ill_all),
         slabs((durables + 1) * ill_rows),
     ] + [
-        dma((n,)) for n in (1, 1, 1, 1, 1, 1, 1, 1, 1, 1, 1, 2, 1, 1, 1, 1, 1, 1)
+        dma((n,)) for n in (1, 1, 1, 1, 1, 1, 1, 1, 1, 1, 2, 1, 1, 1, 1, 1, 1)
     ] + [pltpu.SemaphoreType.REGULAR]
 
 

time: 16.6 us -> 16.5 us (level)
  no operation moved by 1% of the time
where the time goes in v6:
time: 16.5 us; the launch traced here: 16.3 us
  Pallas kernels  15.6 us (95%)
  between operations  0.64 us (4%)
    pallas_call x1, Pallas kernels, body(): pl.pallas_call(functools.partial(step_kernel, dims), out_shape=(held, hel...  15 us
    pallas_call x1, Pallas kernels, body(): pl.pallas_call(store, out_shape=(result, result), in_specs=[vmem, vmem],...  0.67 us

profile of v6, /device:TPU:0, one launch (start us, length us, event | category | flops | bytes accessed | tf_op | source)
XLA Modules:
  0.0 16.3 jit_solution(17670246450343794432)
XLA Ops:
  0.6 15.0 %transposed_window.1 = (f32[128,128]{1,0:T(8,128)S(1)}, f32[128,128]{1,0:T(8,128)S(1)}) custom-call(f32[128,128]{1,0:T(8,128)} %bitcast.13, f32[32,32]{1,0:T(8,128)} %transition_hbm.1, f32[1,32]{1,0:T(1,128)} %bitcast.21, f32[2]{0:T(128)} %drift_hbm.1, f32[2]{0:T(128)} %keep_hbm.1, s32[128,128]{1,0:T(8,128)} %bitcast.14, f32[128,128]{1,0:T(8,128)} %bitcast.15, ...), custom_call_target="tpu_custom_call" | custom-call | tf_op jit(solution)/shard_map/transposed_window/pallas_call | solution.py:1106
  15.6 0.7 %store.1 = (f32[128,128]{1,0:T(8,128)}, f32[128,128]{1,0:T(8,128)}) custom-call(f32[128,128]{1,0:T(8,128)S(1)} %get-tuple-element.6.consumption_ref, f32[128,128]{1,0:T(8,128)S(1)} %get-tuple-element.7.next_ref), custom_call_target="tpu_custom_call" | custom-call | tf_op jit(solution)/shard_map/store/pallas_call | solution.py:1128

commit v7 on v6

--- a/solution.py
+++ b/solution.py
@@ -533,75 +533,6 @@
     for d in range(durables):
         side_out[d, ill_rows] = drifts
 
-    with scope("bar"):
-        dur_peers = jnp.minimum(dur_me, 1) + jnp.minimum(dur_n - 1 - dur_me, 1)
-        pl.semaphore_wait(barrier, len(peers) + dur_peers)
-
-    @pl.when((dur_me < dur_n - 1) & (ill_me == 0))
-    def _():
-        pl.semaphore_signal(ready_sem, inc=1, device_id={"dur": dur_me + 1}, device_id_type=MESH_ID)
-
-    def bundle_copy(out_ref, in_ref, send, recv, first, count, step, i):
-        liq_there, kept = peer_of(liq_me, step, liq_n), pl.ds(first, count)
-        return pltpu.make_async_remote_copy(
-            src_ref=out_ref.at[i * liq_n + liq_there, kept], dst_ref=in_ref.at[liq_me * ill_n + ill_me, kept],
-            send_sem=send.at[0], recv_sem=recv.at[0], device_id={"liq": liq_there, "ill": i}, device_id_type=MESH_ID,
-        )
-
-    def bundle_all(out_ref, in_ref, send, recv, first, count):
-        span, kept = pl.ds(0, len(peers)), pl.ds(first, count)
-        return pltpu.make_async_remote_copy(
-            src_ref=out_ref.at[span, kept], dst_ref=in_ref.at[span, kept], send_sem=send.at[0], recv_sem=recv.at[0],
-            device_id=at(0, 1), device_id_type=MESH_ID,
-        )
-
-    def near_all():
-        return bundle_all(near_out, near_in, near_send, near_recv, 0, per_dest)
-
-    def late_all():
-        return bundle_all(late_out, late_in, late_send, late_recv, 0, 2 * ill_rows)
-
-    def goal_all():
-        return bundle_all(late_out, late_in, late_send, goal_recv, 2 * ill_rows, ill_rows)
-
-    def near_copy(step, i):
-        return bundle_copy(near_out, near_in, near_send, near_recv, 0, per_dest, step, i)
-
-    def late_copy(step, i):
-        return bundle_copy(late_out, late_in, late_send, late_recv, 0, 2 * ill_rows, step, i)
-
-    def goal_copy(step, i):
-        return bundle_copy(late_out, late_in, late_send, goal_recv, 2 * ill_rows, ill_rows, step, i)
-
-    def side_copy(flip):
-        there = at(0, flip)
-        return pltpu.make_async_remote_copy(
-            src_ref=side_out.at[there["ill"]], dst_ref=side_in.at[ill_me],
-            send_sem=side_send.at[flip - 1], recv_sem=side_recv.at[flip - 1], device_id=there, device_id_type=MESH_ID,
-        )
-
-    def pair_copy(flip):
-        there = at(0, flip)
-        return pltpu.make_async_remote_copy(
-            src_ref=near_out.at[pl.ds(there["ill"] * liq_n, liq_n), pl.ds(ill_rows, 2 * ill_rows)],
-            dst_ref=pair_in.at[ill_me], send_sem=pair_send.at[flip - 1], recv_sem=pair_recv.at[flip - 1],
-            device_id=there, device_id_type=MESH_ID,
-        )
-
-    def start_far(i, make):
-        make(liq_n - 1, i).start()
-
-    def start_close(i, make):
-        for step in range(liq_n - 2, 0, -1):
-            make(step, i).start()
-
-        @pl.when(ill_me != i)
-        def _():
-            make(0, i).start()
-
-    for flip in range(1, ill_n):
-        side_copy(flip).start()
-
     load_all(6, 4)
     loads[11].wait()
     for d, a in kinds:
@@ -610,6 +541,75 @@
             late_out[d * liq_n + q, a] = lottery_ref[span, :] - SLOPE_GAIN * steady_ref[span, :]
             late_out[d * liq_n + q, ill_rows + a] = population_ref[span, :]
             late_out[d * liq_n + q, 2 * ill_rows + a] = target_ref[span, :].astype(f32)
+    with scope("bar"):
+        dur_peers = jnp.minimum(dur_me, 1) + jnp.minimum(dur_n - 1 - dur_me, 1)
+        pl.semaphore_wait(barrier, len(peers) + dur_peers)
+
+    @pl.when((dur_me < dur_n - 1) & (ill_me == 0))
+    def _():
+        pl.semaphore_signal(ready_sem, inc=1, device_id={"dur": dur_me + 1}, device_id_type=MESH_ID)
+
+    def bundle_copy(out_ref, in_ref, send, recv, first, count, step, i):
+        liq_there, kept = peer_of(liq_me, step, liq_n), pl.ds(first, count)
+        return pltpu.make_async_remote_copy(
+            src_ref=out_ref.at[i * liq_n + liq_there, kept], dst_ref=in_ref.at[liq_me * ill_n + ill_me, kept],
+            send_sem=send.at[0], recv_sem=recv.at[0], device_id={"liq": liq_there, "ill": i}, device_id_type=MESH_ID,
+        )
+
+    def bundle_all(out_ref, in_ref, send, recv, first, count):
+        span, kept = pl.ds(0, len(peers)), pl.ds(first, count)
+        return pltpu.make_async_remote_copy(
+            src_ref=out_ref.at[span, kept], dst_ref=in_ref.at[span, kept], send_sem=send.at[0], recv_sem=recv.at[0],
+            device_id=at(0, 1), device_id_type=MESH_ID,
+        )
+
+    def near_all():
+        return bundle_all(near_out, near_in, near_send, near_recv, 0, per_dest)
+
+    def late_all():
+        return bundle_all(late_out, late_in, late_send, late_recv, 0, 2 * ill_rows)
+
+    def goal_all():
+        return bundle_all(late_out, late_in, late_send, goal_recv, 2 * ill_rows, ill_rows)
+
+    def near_copy(step, i):
+        return bundle_copy(near_out, near_in, near_send, near_recv, 0, per_dest, step, i)
+
+    def late_copy(step, i):
+        return bundle_copy(late_out, late_in, late_send, late_recv, 0, 2 * ill_rows, step, i)
+
+    def goal_copy(step, i):
+        return bundle_copy(late_out, late_in, late_send, goal_recv, 2 * ill_rows, ill_rows, step, i)
+
+    def side_copy(flip):
+        there = at(0, flip)
+        return pltpu.make_async_remote_copy(
+            src_ref=side_out.at[there["ill"]], dst_ref=side_in.at[ill_me],
+            send_sem=side_send.at[flip - 1], recv_sem=side_recv.at[flip - 1], device_id=there, device_id_type=MESH_ID,
+        )
+
+    def pair_copy(flip):
+        there = at(0, flip)
+        return pltpu.make_async_remote_copy(
+            src_ref=near_out.at[pl.ds(there["ill"] * liq_n, liq_n), pl.ds(ill_rows, 2 * ill_rows)],
+            dst_ref=pair_in.at[ill_me], send_sem=pair_send.at[flip - 1], recv_sem=pair_recv.at[flip - 1],
+            device_id=there, device_id_type=MESH_ID,
+        )
+
+    def start_far(i, make):
+        make(liq_n - 1, i).start()
+
+    def start_close(i, make):
+        for step in range(liq_n - 2, 0, -1):
+            make(step, i).start()
+
+        @pl.when(ill_me != i)
+        def _():
+            make(0, i).start()
+
+    for flip in range(1, ill_n):
+        side_copy(flip).start()
+
     start_far(0, near_copy)
     start_far(0, goal_copy)
     start_close(0, near_copy)

time: 16.5 us -> 16.5 us (level)
  no operation moved by 1% of the time
where the time goes in v7:
time: 16.5 us; the launch traced here: 16.2 us
  Pallas kernels  15.6 us (95%)
  between operations  0.64 us (4%)
    pallas_call x1, Pallas kernels, body(): pl.pallas_call(functools.partial(step_kernel, dims), out_shape=(held, hel...  14.9 us
    pallas_call x1, Pallas kernels, body(): pl.pallas_call(store, out_shape=(result, result), in_specs=[vmem, vmem],...  0.67 us

profile of v7, /device:TPU:0, one launch (start us, length us, event | category | flops | bytes accessed | tf_op | source)
XLA Modules:
  0.0 16.2 jit_solution(3568378286001767819)
XLA Ops:
  0.6 14.9 %transposed_window.1 = (f32[128,128]{1,0:T(8,128)S(1)}, f32[128,128]{1,0:T(8,128)S(1)}) custom-call(f32[128,128]{1,0:T(8,128)} %bitcast.13, f32[32,32]{1,0:T(8,128)} %transition_hbm.1, f32[1,32]{1,0:T(1,128)} %bitcast.21, f32[2]{0:T(128)} %drift_hbm.1, f32[2]{0:T(128)} %keep_hbm.1, s32[128,128]{1,0:T(8,128)} %bitcast.14, f32[128,128]{1,0:T(8,128)} %bitcast.15, ...), custom_call_target="tpu_custom_call" | custom-call | tf_op jit(solution)/shard_map/transposed_window/pallas_call | solution.py:1106
  15.6 0.7 %store.1 = (f32[128,128]{1,0:T(8,128)}, f32[128,128]{1,0:T(8,128)}) custom-call(f32[128,128]{1,0:T(8,128)S(1)} %get-tuple-element.6.consumption_ref, f32[128,128]{1,0:T(8,128)S(1)} %get-tuple-element.7.next_ref), custom_call_target="tpu_custom_call" | custom-call | tf_op jit(solution)/shard_map/store/pallas_call | solution.py:1128
